TPU v7x, 32 devices: a whole 2x2x4 slice. The times are simulated.
32 devices in a mesh: cube: 2 (over x), chan: 8 (over z, y), split: 2 (over core).
Axes of the slice: x: 2, y: 2, z: 4, core: 2. Of those that a mesh axis runs over, the one named last changes fastest.
Arguments:
- sky_image: bfloat16 [16, 8, 1, 2, 512, 128], P(('cube', 'chan'), None, None, 'split'), parts along dimension 0, may hold values from 0 to 8
- dirty_image: bfloat16 [16, 8, 1, 2, 512, 128], P(('cube', 'chan'), None, None, 'split'), parts along dimension 0, may hold values from -6 to 6
- uv_weights: int32 [16, 1024, 512], P(('cube', 'chan'), 'split'), parts along dimension 0, may hold values from 0 to 7
- dual_coeffs: bfloat16 [4, 16, 8, 2, 512, 128], P(None, 'cube', 'chan', 'split'), parts along dimension 1, may hold values from -3 to 3
- support_mask: int32 [8, 2, 512, 128], P('chan', 'split'), may hold values 0 or 1
- row_taps: float32 [4, 17], replicated, may hold values from -1.5 to 1.5
- col_taps: float32 [4, 17], replicated, may hold values from -1.5 to 1.5
Outputs:
- new_image: bfloat16 [16, 8, 1, 2, 512, 128], P(('cube', 'chan'), None, None, 'split'), parts along dimension 0
- new_dual: bfloat16 [4, 16, 8, 2, 512, 128], P(None, 'cube', 'chan', 'split'), parts along dimension 1
There are 2 independent parts, one for each index of `cube`. A program takes and returns all parts, laid end to end along the dimension named above; an argument that names none is the same for every part. Nothing has to cross between parts.
All inputs are finite; a program needn't handle non-finite values. No bound on the sum of `support_mask` on one device may be relied on, other than what follows from the above.
Results may differ from a plain program's by a relative error of at most 0.015.
Values may be sent and summed in bfloat16 or wider, within the bound.
A program may use at most 128 MiB of HBM per device.

v0:
```python
import functools
import math

import jax
import jax.numpy as jnp
from jax import lax
from jax.experimental import pallas as pl
from jax.experimental.pallas import tpu as pltpu
from jax.sharding import PartitionSpec as P

NB = 4
TAPS = 17
MARGIN = 8
PAD = 16

primal_step = 0.5
dual_step = 0.5
radius = 6.0
weight_unit = 0.25
f32 = jnp.float32
bf16 = jnp.bfloat16


def dot(a, b):
    return jnp.dot(a, b, preferred_element_type=f32)


def col_dft(npix):
    half = npix // 2
    product = jnp.arange(npix)[:, None] * jnp.arange(half)[None, :] % npix
    phases = product.astype(f32) * (2.0 * math.pi / npix)
    factor = 1.0 / math.sqrt(npix)
    return jnp.concatenate(
        [(jnp.cos(phases) * factor).astype(bf16), (-jnp.sin(phases) * factor).astype(bf16)], axis=1
    )


def side_cols(k, width):
    return jnp.where(k < MARGIN, k - MARGIN, width - MARGIN + k)


def toeplitz(taps, index):
    out = jnp.zeros((NB,) + index.shape, f32)
    for t in range(TAPS):
        out = jnp.where(index[None] == t, taps[:, t][:, None, None], out)
    return out


def adjoint_tables(row_taps, col_taps, width, block):
    h = row_taps.astype(bf16).astype(f32)
    g = col_taps.astype(bf16).astype(f32)
    i = jnp.arange(width)[:, None]
    j = jnp.arange(width)[None, :]
    main = toeplitz(g, j - i + MARGIN)
    k = jnp.arange(width)[None, :]
    side_index = jnp.where(k < 2 * MARGIN, side_cols(k, width) - i + MARGIN, -1)
    side = toeplitz(g, side_index)
    cols = jnp.concatenate([main, side], axis=2).astype(bf16)
    r = jnp.arange(block)[:, None]
    w = jnp.arange(NB * (block + 2 * PAD))[None, :]
    span = block + 2 * PAD
    rows = jnp.zeros((block, NB * span), f32)
    index = r - w % span + PAD + MARGIN
    for t in range(TAPS):
        tap_row = jnp.repeat(h[:, t], span)[None, :]
        rows = jnp.where(index == t, tap_row, rows)
    return cols, rows.astype(bf16)


def forward_tables(row_taps, col_taps, width, block):
    h = row_taps.astype(bf16).astype(f32)
    g = col_taps.astype(bf16).astype(f32)
    i = jnp.arange(width)[:, None]
    j = jnp.arange(NB * width)[None, :]
    main_index = i - j % width + MARGIN
    side_index = jnp.where(i < 2 * MARGIN, side_cols(i, width) - j % width + MARGIN, -1)
    index = jnp.concatenate([main_index, side_index], axis=0)
    cols = jnp.zeros(index.shape, f32)
    for t in range(TAPS):
        tap_row = jnp.repeat(g[:, t], width)[None, :]
        cols = jnp.where(index == t, tap_row, cols)
    r = jnp.arange(block)[:, None]
    w = jnp.arange(block + 2 * PAD)[None, :]
    rows = toeplitz(h, w - r - PAD + MARGIN)
    return cols.astype(bf16), rows.astype(bf16)


def spill_tables(fcols, width):
    span = 2 * MARGIN
    row = jnp.arange(fcols * span)[:, None]
    col = jnp.arange(fcols * width)[None, :]
    rb, rk = row // span, row % span
    gather = jnp.where(rk >= MARGIN, (rb + 1) * width + rk - MARGIN, rb * width - MARGIN + rk)
    table = (gather == col).astype(bf16)
    return table


def adjoint_body(C, R, W, B, u, up, lo, gcols, hrows, adj, adjs, dc, dcs):
    per = W // (2 * MARGIN)
    for n in range(NB):
        main = gcols[n, :, :W]
        side0 = gcols[n, :, W:].astype(f32)
        for c0 in range(0, C, per):
            acc = None
            for cc in range(per):
                c = c0 + cc
                side = pltpu.roll(side0, 2 * MARGIN * cc, 1) if cc else side0
                table = jnp.concatenate([main, side.astype(bf16)], axis=1)
                rows = jnp.concatenate([up[n, c], u[n, c], lo[n, c]], axis=0)
                out = dot(rows, table)
                dc[n, :, c * W : (c + 1) * W] = out[:, :W].astype(bf16)
                acc = out[:, W:] if acc is None else acc + out[:, W:]
            dcs[n, :, c0 * 2 * MARGIN : c0 * 2 * MARGIN + W] = acc.astype(bf16)
    span = B + 2 * PAD
    for k in range(R // B):
        lo_row = k * B
        hr = hrows[...]
        for c in range(0, C, 2):
            win = jnp.concatenate(
                [dc[n, lo_row : lo_row + span, c * W : (c + 2) * W] for n in range(NB)], axis=0
            )
            out = dot(hr, win).astype(bf16)
            adj[c, lo_row : lo_row + B] = out[:, :W]
            adj[c + 1, lo_row : lo_row + B] = out[:, W:]
        for c0 in range(0, C, per):
            lanes = c0 * 2 * MARGIN
            win = jnp.concatenate(
                [dcs[n, lo_row : lo_row + span, lanes : lanes + W] for n in range(NB)], axis=0
            )
            out = dot(hr, win).T.astype(bf16)
            for cc in range(per):
                adjs[c0 + cc, :, lo_row : lo_row + B] = out[cc * 16 : cc * 16 + 16]


def half_body(FC, W, x, colT, out):
    full = out.shape[1]
    rows = jnp.concatenate([x[b] for b in range(FC)], axis=1)

    @pl.loop(0, full // 256)
    def _(j):
        lanes = pl.ds(pl.multiple_of(j * 256, 256), 256)
        out[:, lanes] = dot(rows, colT[:, lanes]).astype(bf16)


def table_body(s, FR, R, colT, bown, aown, aoth):
    half = FR * R
    for a in range(FR):
        own = pl.ds(pl.multiple_of((2 * a + s) * R, R), R)
        bown[a * R : (a + 1) * R] = colT[own, :]
    sign_row = lax.broadcasted_iota(jnp.int32, (1, half), 1) % 2
    flip = jnp.where((sign_row == 1) & (s == 1), -1.0, 1.0).astype(f32)
    for dst, part in ((aown, s), (aoth, 1 - s)):
        for q in range(2):
            pieces = [
                colT[pl.ds(pl.multiple_of((2 * a + part) * R, R), R), q * half : (q + 1) * half]
                for a in range(FR)
            ]
            block = jnp.concatenate(pieces, axis=0) if FR > 1 else pieces[0]
            dst[:, q * half : (q + 1) * half] = (block.astype(f32).T * flip).astype(bf16)


def stack_re_im(ref, lanes_re, lanes_im, transpose):
    re, im = ref[:, lanes_re], ref[:, lanes_im]
    if transpose:
        return jnp.concatenate([re, im], 0), jnp.concatenate([im, -re], 0)
    return jnp.concatenate([re, -im], 0), jnp.concatenate([im, re], 0)


def vis_body(half, aown, aoth, hown, hoth, wts, out):
    step = 256

    @pl.loop(0, half // step)
    def _(j):
        re_l = pl.ds(pl.multiple_of(j * step, step), step)
        im_l = pl.ds(pl.multiple_of(j * step + half, step), step)
        own_re, own_im = stack_re_im(hown, re_l, im_l, False)
        oth_re, oth_im = stack_re_im(hoth, re_l, im_l, False)
        scale = weight_unit * wts[:, re_l].astype(f32)
        re = dot(aown[...], own_re) + dot(aoth[...], oth_re)
        out[:, re_l] = (scale * re).astype(bf16)
        im = dot(aown[...], own_im) + dot(aoth[...], oth_im)
        out[:, im_l] = (scale * im).astype(bf16)


def back_body(s, half, bown, wown, woth, out):
    step = 256
    odd = lax.broadcasted_iota(jnp.int32, (half, 1), 0) % 2 == 1
    own_sign = jnp.where(odd & (s == 1), -1.0, 1.0)
    oth_sign = jnp.where(odd & (s == 0), -1.0, 1.0)

    @pl.loop(0, half // step)
    def _(j):
        re_l = pl.ds(pl.multiple_of(j * step, step), step)
        im_l = pl.ds(pl.multiple_of(j * step + half, step), step)
        own_re, own_im = stack_re_im(wown, re_l, im_l, True)
        oth_re, oth_im = stack_re_im(woth, re_l, im_l, True)
        re = own_sign * dot(bown[...], own_re) + oth_sign * dot(bown[...], oth_re)
        out[:, re_l] = re.astype(bf16)
        im = own_sign * dot(bown[...], own_im) + oth_sign * dot(bown[...], oth_im)
        out[:, im_l] = im.astype(bf16)


def image_body(FC, FR, R, W, back, colT, spill, x, d, adj, adjs, new, ext, exts):
    st_rows = []
    for a in range(FR):
        parts = jnp.concatenate([adjs[b * FR + a] for b in range(FC)], axis=0)
        st_rows.append(parts.astype(f32).T.astype(bf16))
    st = jnp.concatenate(st_rows, axis=0) if FR > 1 else st_rows[0]
    es = None
    for b in range(FC):
        cols = slice(b * W, (b + 1) * W)
        grad = lax.dot_general(
            back[...], colT[cols, :], (((1,), (1,)), ((), ())), preferred_element_type=f32
        )
        grad = grad + dot(st, spill[:, cols])
        pieces = [adj[b * FR + a] for a in range(FR)]
        main = jnp.concatenate(pieces, axis=0) if FR > 1 else pieces[0]
        xb = x[b].astype(f32)
        upd = xb - primal_step * (grad - d[b].astype(f32) + main.astype(f32))
        nb = jnp.maximum(upd, 0.0).astype(bf16)
        eb = (2.0 * nb.astype(f32) - xb).astype(bf16)
        new[b] = nb
        for a in range(FR):
            ext[b * FR + a] = eb[a * R : (a + 1) * R]
        part = lax.dot_general(
            eb, spill[:, cols], (((1,), (1,)), ((), ())), preferred_element_type=f32
        )
        es = part if es is None else es + part
    for a in range(FR):
        t = es[a * R : (a + 1) * R].T.astype(bf16)
        for b in range(FC):
            exts[b * FR + a] = t[b * 16 : b * 16 + 16]


def forward_cols_body(C, R, W, main, sides, fcols, ic):
    per = W // 16
    for c0 in range(0, C, per):
        parts = jnp.concatenate([sides[c0 + cc] for cc in range(per)], axis=0)
        st = parts.astype(f32).T.astype(bf16)
        for cc in range(per):
            c = c0 + cc
            zeros_a = jnp.zeros((cc * 16, NB * W), bf16)
            zeros_b = jnp.zeros((W - 16 - cc * 16, NB * W), bf16)
            pieces = [fcols[:W], fcols[W : W + 16]]
            if cc:
                pieces.insert(1, zeros_a)
            if cc < per - 1:
                pieces.append(zeros_b)
            table = jnp.concatenate(pieces, axis=0)
            out = dot(jnp.concatenate([main[c], st], axis=1), table)
            for n in range(NB):
                ic[n, PAD : PAD + R, c * W : (c + 1) * W] = out[:, n * W : (n + 1) * W].astype(bf16)


def shrink_body(C, R, W, B, ic, frows, u, mask, out):
    span = B + 2 * PAD
    for k in range(R // B):
        keep = radius * mask[k * B : (k + 1) * B].astype(f32)
        for n in range(NB):
            hr = frows[n]
            coef = dot(hr, ic[n, k * B : k * B + span])
            total = None
            steps = []
            for c in range(C):
                st = u[n, c, k * B : (k + 1) * B].astype(f32) + dual_step * coef[:, c * W : (c + 1) * W]
                steps.append(st)
                total = st * st if total is None else total + st * st
            scale = keep / jnp.maximum(jnp.sqrt(total), radius)
            for c in range(C):
                out[n, c, k * B : (k + 1) * B] = (steps[c] * scale).astype(bf16)


def call(body, outs, scratch=(), flops=10**9):
    params = pltpu.CompilerParams(vmem_limit_bytes=60 * 2**20)
    return pl.pallas_call(
        body,
        out_shape=[jax.ShapeDtypeStruct(o, bf16) for o in outs],
        scratch_shapes=[pltpu.VMEM(x, bf16) for x in scratch],
        compiler_params=params,
        cost_estimate=pl.CostEstimate(flops=flops, bytes_accessed=4 * 2**20, transcendentals=0),
    )


def per_device(sky_image, dirty_image, uv_weights, dual_coeffs, support_mask, row_taps, col_taps):
    FC, FR = sky_image.shape[1], sky_image.shape[2]
    R, W = sky_image.shape[4], sky_image.shape[5]
    C = dual_coeffs.shape[1]
    npix = FC * W
    half = npix // 2
    B = min(128, R)
    RP = R + 2 * PAD
    s = lax.axis_index("split")
    u = dual_coeffs.reshape(NB, C, R, W)
    x = sky_image.reshape(FC, FR * R, W)
    d = dirty_image.reshape(FC, FR * R, W)
    wts = uv_weights.reshape(half, half)
    mask = support_mask.reshape(R, W)
    colT = col_dft(npix)
    spill = spill_tables(FC, W)
    chain = ("chan", "split")
    count = lax.axis_size(chain)
    down = [(i, i + 1) for i in range(count) if (i + 1) % (2 * FR)]
    upward = [(i + 1, i) for i in range(count) if (i + 1) % (2 * FR)]
    swap = [(0, 1), (1, 0)]

    up = lax.ppermute(u[:, :, R - PAD :], chain, down)
    lo = lax.ppermute(u[:, :, :PAD], chain, upward)
    gcols, hrows = adjoint_tables(row_taps, col_taps, W, B)
    adj, adjs = call(
        functools.partial(adjoint_body, C, R, W, B),
        [(C, R, W), (C, 16, R)],
        [(NB, RP, C * W), (NB, RP, C * 16)],
    )(u, up, lo, gcols, hrows)
    adj = lax.all_to_all(adj, "chan", 0, 0, tiled=True)
    adjs = lax.all_to_all(adjs, "chan", 0, 0, tiled=True)

    (hown,) = call(functools.partial(half_body, FC, W), [(half, npix)])(x, colT)
    hoth = lax.ppermute(hown, "split", swap)

    def tables(colT_ref, bown, aown, aoth):
        table_body(lax.axis_index("split"), FR, R, colT_ref, bown, aown, aoth)

    bown, aown, aoth = call(tables, [(half, npix)] * 3)(colT)
    (wown,) = call(functools.partial(vis_body, half), [(half, npix)])(aown, aoth, hown, hoth, wts)
    woth = lax.ppermute(wown, "split", swap)

    def back_call(*refs):
        back_body(lax.axis_index("split"), half, *refs)

    (back,) = call(back_call, [(half, npix)])(bown, wown, woth)
    new, ext, exts = call(
        functools.partial(image_body, FC, FR, R, W),
        [(FC, FR * R, W), (C, R, W), (C, 16, R)],
    )(back, colT, spill, x, d, adj, adjs)
    main = lax.all_to_all(ext, "chan", 0, 0, tiled=True)
    sides = lax.all_to_all(exts, "chan", 0, 0, tiled=True)
    fcols, frows = forward_tables(row_taps, col_taps, W, B)

    def fcall(main, sides, fcols, ic):
        forward_cols_body(C, R, W, main, sides, fcols, ic)

    (ic,) = call(fcall, [(NB, RP, C * W)])(main, sides, fcols)
    top = lax.ppermute(ic[:, R : R + PAD], chain, down)
    bottom = lax.ppermute(ic[:, PAD : 2 * PAD], chain, upward)

    def scall(ic, top, bottom, frows, u, mask, out, ics):
        ics[:, :PAD] = top[...]
        ics[:, PAD : PAD + R] = ic[:, PAD : PAD + R]
        ics[:, PAD + R :] = bottom[...]
        shrink_body(C, R, W, B, ics, frows, u, mask, out)

    (new_dual,) = call(scall, [(NB, C, R, W)], [(NB, RP, C * W)])(ic, top, bottom, frows, u, mask)
    return (new.reshape(sky_image.shape), new_dual.reshape(dual_coeffs.shape))


def solution(mesh):
    placed = (
        P(("cube", "chan"), None, None, "split", None, None),
        P(("cube", "chan"), None, None, "split", None, None),
        P(("cube", "chan"), "split", None),
        P(None, "cube", "chan", "split", None, None),
        P("chan", "split", None, None),
        P(),
        P(),
    )
    return jax.shard_map(
        per_device,
        mesh=mesh,
        in_specs=placed,
        out_specs=(
            P(("cube", "chan"), None, None, "split", None, None),
            P(None, "cube", "chan", "split", None, None),
        ),
        check_vma=False,
    )
```

profile of v0, /device:TPU:0, one launch (start us, length us, event | category | flops | bytes accessed | tf_op | source)
XLA Modules:
  0.0 149.6 jit_solution(14538774417378079044)
XLA Ops:
  0.6 8.6 %multiply_convert_fusion = (bf16[1024,512]{1,0:T(8,128)(2,1)S(1)}, bf16[1024,512]{1,0:T(8,128)(2,1)S(1)}) fusion(), kind=kLoop, calls=%fused_computation.7 | loop fusion | flops 9961472 | bytes 2097152 | tf_op jit(solution)/shard_map/convert_element_type | solution.py:34
  9.2 1.6 %pad_maximum_fusion.colT_ref.colT = bf16[1024,1024]{1,0:T(8,128)(2,1)} fusion(bf16[1024,512]{1,0:T(8,128)(2,1)S(1)} %get-tuple-element.77, bf16[1024,512]{1,0:T(8,128)(2,1)S(1)} %get-tuple-element.78), kind=kLoop, calls=%fused_computation.6 | loop fusion | flops 4194304 | bytes 4194304 | tf_op jit(solution)/shard_map/concatenate | solution.py:33
  10.8 4.8 %shard_map.87.hown = bf16[512,1024]{1,0:T(8,128)(2,1)} custom-call(bf16[8,512,128]{2,1,0:T(8,128)(2,1)} %bitcast.49, bf16[1024,1024]{1,0:T(8,128)(2,1)} %pad_maximum_fusion.colT_ref.colT), custom_call_target="tpu_custom_call" | custom-call | flops 1000000000 | bytes 4194304 | tf_op jit(solution)/shard_map/pallas_call | solution.py:317
  15.7 0.5 collective-permute-start
  16.2 1.0 fusion.82
  17.1 1.9 %collective-permute-start.2 = (bf16[4,8,16,128]{3,2,1,0:T(8,128)(2,1)S(1)}, bf16[4,8,16,128]{3,2,1,0:T(8,128)(2,1)S(1)}, u32[]{:S(2)}, u32[]{:S(2)}) collective-permute-start(bf16[4,8,16,128]{3,2,1,0:T(8,128)(2,1)S(1)} %get-tuple-element.57), channel_id=1, source_target_pairs={{0,1},{2,3},{4,5},{6,7},{8,9},{10,11},{12,13},{14,15},{16,17},{18,... | collective-permute-start | bytes 393224 | tf_op jit(solution)/shard_map/ppermute | solution.py:306
  19.1 1.3 collective-permute-start.3
  20.7 0.5 slice_reduce_fusion.33
  21.2 0.5 slice_reduce_fusion.16
  21.8 0.1 broadcast_in_dim.1116
  22.0 0.1 broadcast_in_dim.1113
  24.5 0.2 fusion.57
  24.7 0.6 select_convert_fusion.3
  25.3 0.6 select_convert_fusion.4
  25.9 1.1 select_convert_fusion.2.hrows
  27.0 0.7 pad_maximum_fusion.1.gcols
  27.7 0.6 copy-done.6
  28.4 0.6 copy-done.7
  29.0 6.9 %shard_map.90 = (bf16[8,512,128]{2,1,0:T(8,128)(2,1)}, bf16[8,16,512]{2,1,0:T(8,128)(2,1)}) custom-call(bf16[4,8,512,128]{3,2,1,0:T(8,128)(2,1)} %bitcast.46, bf16[4,8,16,128]{3,2,1,0:T(8,128)(2,1)} %copy-done.6, bf16[4,8,16,128]{3,2,1,0:T(8,128)(2,1)} %copy-done.7, bf16[4,128,256]{2,1,0:T(8,128)(2,1)} %pad_maximum_fusion.1.gcols, ...), custom_call_target="tpu_custom_call" | custom-call | flops 1000000000 | bytes 4194304 | tf_op jit(solution)/shard_map/pallas_call | solution.py:309
  35.9 7.3 %all-to-all-start.1 = ((bf16[8,16,512]{2,1,0:T(8,128)(2,1)}), bf16[8,16,512]{2,1,0:T(8,128)(2,1)S(1)}, u32[]{:S(2)}, u32[]{:S(2)}) async-start(bf16[8,16,512]{2,1,0:T(8,128)(2,1)} %get-tuple-element.14), calls=%async_computation.1 | async-start | bytes 262144 | tf_op jit(solution)/shard_map/all_to_all | solution.py:315
  43.3 8.2 %all-to-all-done.1.adjs = bf16[8,16,512]{2,1,0:T(8,128)(2,1)S(1)} async-done(((bf16[8,16,512]{2,1,0:T(8,128)(2,1)}), bf16[8,16,512]{2,1,0:T(8,128)(2,1)S(1)}, u32[]{:S(2)}, u32[]{:S(2)}) %all-to-all-start.1) | async-done | bytes 131104 | tf_op jit(solution)/shard_map/all_to_all | solution.py:315
  51.4 3.7 %all-to-all-start = ((bf16[8,512,128]{2,1,0:T(8,128)(2,1)}), bf16[8,512,128]{2,1,0:T(8,128)(2,1)S(1)}, u32[]{:S(2)}, u32[]{:S(2)}) async-start(bf16[8,512,128]{2,1,0:T(8,128)(2,1)} %get-tuple-element.13), calls=%async_computation | async-start | bytes 2097152 | tf_op jit(solution)/shard_map/all_to_all | solution.py:314
  55.2 3.6 %shard_map.86 = (bf16[512,1024]{1,0:T(8,128)(2,1)}, bf16[512,1024]{1,0:T(8,128)(2,1)}, bf16[512,1024]{1,0:T(8,128)(2,1)}) custom-call(bf16[1024,1024]{1,0:T(8,128)(2,1)} %pad_maximum_fusion.colT_ref.colT), custom_call_target="tpu_custom_call" | custom-call | flops 1000000000 | bytes 4194304 | tf_op jit(solution)/shard_map/pallas_call | solution.py:323
  59.0 1.0 copy-done.2
  60.0 6.1 %shard_map.88.refs_1_ = bf16[512,1024]{1,0:T(8,128)(2,1)} custom-call(bf16[512,1024]{1,0:T(8,128)(2,1)} %get-tuple-element.11.aown, bf16[512,1024]{1,0:T(8,128)(2,1)} %get-tuple-element.12.aoth, bf16[512,1024]{1,0:T(8,128)(2,1)} %shard_map.87.hown, bf16[512,1024]{1,0:T(8,128)(2,1)} %copy-done.2, s32[512,512]{1,0:T(8,128)} %bitcast.52), custom_call_target="tpu_custom_call" | custom-call | flops 1000000000 | bytes 4194304 | tf_op jit(solution)/shard_map/pallas_call | solution.py:324
  66.3 0.8 fusion.6.spill
  67.1 1.8 %collective-permute-done.1.refs_2_ = bf16[512,1024]{1,0:T(8,128)(2,1)S(1)} collective-permute-done((bf16[512,1024]{1,0:T(8,128)(2,1)}, bf16[512,1024]{1,0:T(8,128)(2,1)S(1)}, u32[]{:S(2)}, u32[]{:S(2)}) %collective-permute-start.1) | collective-permute-done | bytes 1048608 | tf_op jit(solution)/shard_map/ppermute | solution.py:325
  68.9 1.0 copy-done.3
  69.9 5.5 %shard_map.89.back = bf16[512,1024]{1,0:T(8,128)(2,1)} custom-call(bf16[512,1024]{1,0:T(8,128)(2,1)} %get-tuple-element.10.refs_0_, bf16[512,1024]{1,0:T(8,128)(2,1)} %shard_map.88.refs_1_, bf16[512,1024]{1,0:T(8,128)(2,1)} %copy-done.3), custom_call_target="tpu_custom_call" | custom-call | flops 1000000000 | bytes 4194304 | tf_op jit(solution)/shard_map/pallas_call | solution.py:330
  75.4 5.6 %all-to-all-done.adj = bf16[8,512,128]{2,1,0:T(8,128)(2,1)S(1)} async-done(((bf16[8,512,128]{2,1,0:T(8,128)(2,1)}), bf16[8,512,128]{2,1,0:T(8,128)(2,1)S(1)}, u32[]{:S(2)}, u32[]{:S(2)}) %all-to-all-start) | async-done | bytes 1048608 | tf_op jit(solution)/shard_map/all_to_all | solution.py:314
  81.0 1.0 copy-done
  82.0 7.4 %shard_map.91 = (bf16[8,512,128]{2,1,0:T(8,128)(2,1)}, bf16[8,512,128]{2,1,0:T(8,128)(2,1)}, bf16[8,16,512]{2,1,0:T(8,128)(2,1)}) custom-call(bf16[512,1024]{1,0:T(8,128)(2,1)} %shard_map.89.back, bf16[1024,1024]{1,0:T(8,128)(2,1)} %pad_maximum_fusion.colT_ref.colT, bf16[128,1024]{1,0:T(8,128)(2,1)} %fusion.6.spill, bf16[8,512,128]{2,1,0:T(8,128)(2,1)} %bitcast.50, ...), custom_call_target="tpu_custom_call" | custom-call | flops 1000000000 | bytes 4194304 | tf_op jit(solution)/shard_map/pallas_call | solution.py:331
  89.4 3.6 %all-to-all-start.3 = ((bf16[8,16,512]{2,1,0:T(8,128)(2,1)}), bf16[8,16,512]{2,1,0:T(8,128)(2,1)S(1)}, u32[]{:S(2)}, u32[]{:S(2)}) async-start(bf16[8,16,512]{2,1,0:T(8,128)(2,1)} %get-tuple-element.17), calls=%async_computation.3 | async-start | bytes 262144 | tf_op jit(solution)/shard_map/all_to_all | solution.py:336
  93.1 7.3 %all-to-all-done.3.sides = bf16[8,16,512]{2,1,0:T(8,128)(2,1)S(1)} async-done(((bf16[8,16,512]{2,1,0:T(8,128)(2,1)}), bf16[8,16,512]{2,1,0:T(8,128)(2,1)S(1)}, u32[]{:S(2)}, u32[]{:S(2)}) %all-to-all-start.3) | async-done | bytes 131104 | tf_op jit(solution)/shard_map/all_to_all | solution.py:336
  100.4 3.6 %all-to-all-start.2 = ((bf16[8,512,128]{2,1,0:T(8,128)(2,1)}), bf16[8,512,128]{2,1,0:T(8,128)(2,1)S(1)}, u32[]{:S(2)}, u32[]{:S(2)}) async-start(bf16[8,512,128]{2,1,0:T(8,128)(2,1)} %get-tuple-element.16), calls=%async_computation.2 | async-start | bytes 2097152 | tf_op jit(solution)/shard_map/all_to_all | solution.py:335
  104.4 0.1 subtract_add_fusion.1
  104.5 1.3 select_convert_fusion.1.fcols
  105.8 23.1 %all-to-all-done.2.main = bf16[8,512,128]{2,1,0:T(8,128)(2,1)S(1)} async-done(((bf16[8,512,128]{2,1,0:T(8,128)(2,1)}), bf16[8,512,128]{2,1,0:T(8,128)(2,1)S(1)}, u32[]{:S(2)}, u32[]{:S(2)}) %all-to-all-start.2) | async-done | bytes 1048608 | tf_op jit(solution)/shard_map/all_to_all | solution.py:335
  128.9 1.0 copy-done.1
  129.8 4.9 %shard_map.92.ic = bf16[4,544,1024]{2,1,0:T(8,128)(2,1)} custom-call(bf16[8,512,128]{2,1,0:T(8,128)(2,1)} %copy-done.1, bf16[8,16,512]{2,1,0:T(8,128)(2,1)} %copy-done.4, bf16[256,512]{1,0:T(8,128)(2,1)} %select_convert_fusion.1.fcols), custom_call_target="tpu_custom_call" | custom-call | flops 1000000000 | bytes 4194304 | tf_op jit(solution)/shard_map/pallas_call | solution.py:342
  134.7 1.0 fusion.81
  135.7 1.3 collective-permute-start.4
  137.0 1.3 collective-permute-start.5
  138.3 1.5 select_convert_fusion.frows
  139.8 0.5 collective-permute-done.5.bottom
  140.2 0.2 copy-done.8
  140.4 0.5 copy-done.9
  140.9 8.7 %shard_map.93 = bf16[4,8,512,128]{3,2,1,0:T(8,128)(2,1)} custom-call(bf16[4,544,1024]{2,1,0:T(8,128)(2,1)} %shard_map.92.ic, bf16[4,16,1024]{2,1,0:T(8,128)(2,1)} %copy-done.8, bf16[4,16,1024]{2,1,0:T(8,128)(2,1)} %copy-done.9, bf16[4,128,160]{2,1,0:T(8,128)(2,1)} %select_convert_fusion.frows, bf16[4,8,512,128]{3,2,1,0:T(8,128)(2,1)} %bitcast.47, ...), custom_call_target="tpu_custom_call" | custom-call | flops 1000000000 | bytes 4194304 | tf_op jit(solution)/shard_map/pallas_call | solution.py:352
  (87 shorter events, 3.9 us)
Async XLA Ops:
  10.8 9.9 %copy-start.10 = (f32[4,17]{1,0:T(4,128)S(1)}, f32[4,17]{1,0:T(4,128)}, u32[]{:S(2)}) copy-start(f32[4,17]{1,0:T(4,128)} %param.13) | copy-start | bytes 820
  10.8 10.4 %copy-start.11 = (f32[4,17]{1,0:T(4,128)S(1)}, f32[4,17]{1,0:T(4,128)}, u32[]{:S(2)}) copy-start(f32[4,17]{1,0:T(4,128)} %param.12) | copy-start | bytes 820
  15.7 43.3 %collective-permute-start = (bf16[512,1024]{1,0:T(8,128)(2,1)}, bf16[512,1024]{1,0:T(8,128)(2,1)S(1)}, u32[]{:S(2)}, u32[]{:S(2)}) collective-permute-start(bf16[512,1024]{1,0:T(8,128)(2,1)} %shard_map.87.hown), channel_id=1, source_target_pairs={{0,1},{1,0},{2,3},{3,2},{4,5},{5,4},{6,7},{7,6},{8,9},{9,8},{10,11... | collective-permute-start | bytes 3145736 | tf_op jit(solution)/shard_map/ppermute | solution.py:318
  17.1 10.6 %collective-permute-start.2 = (bf16[4,8,16,128]{3,2,1,0:T(8,128)(2,1)S(1)}, bf16[4,8,16,128]{3,2,1,0:T(8,128)(2,1)S(1)}, u32[]{:S(2)}, u32[]{:S(2)}) collective-permute-start(bf16[4,8,16,128]{3,2,1,0:T(8,128)(2,1)S(1)} %get-tuple-element.57), channel_id=1, source_target_pairs={{0,1},{2,3},{4,5},{6,7},{8,9},{10,11},{12,13},{14,15},{16,17},{18,... | collective-permute-start | bytes 393224 | tf_op jit(solution)/shard_map/ppermute | solution.py:306
  19.1 8.6 %collective-permute-start.3 = (bf16[4,8,16,128]{3,2,1,0:T(8,128)(2,1)S(1)}, bf16[4,8,16,128]{3,2,1,0:T(8,128)(2,1)S(1)}, u32[]{:S(2)}, u32[]{:S(2)}) collective-permute-start(bf16[4,8,16,128]{3,2,1,0:T(8,128)(2,1)S(1)} %get-tuple-element.56), channel_id=1, source_target_pairs={{1,0},{3,2},{5,4},{7,6},{9,8},{11,10},{13,12},{15,14},{17,16},{19,... | collective-permute-start | bytes 393224 | tf_op jit(solution)/shard_map/ppermute | solution.py:307
  27.7 0.7 copy-start.6
  28.4 0.6 copy-start.7
  35.9 15.5 %all-to-all-start.1 = ((bf16[8,16,512]{2,1,0:T(8,128)(2,1)}), bf16[8,16,512]{2,1,0:T(8,128)(2,1)S(1)}, u32[]{:S(2)}, u32[]{:S(2)}) async-start(bf16[8,16,512]{2,1,0:T(8,128)(2,1)} %get-tuple-element.14), calls=%async_computation.1 | async-start | bytes 262144 | tf_op jit(solution)/shard_map/all_to_all | solution.py:315
  51.4 7.4 %copy-start.5 = (bf16[8,16,512]{2,1,0:T(8,128)(2,1)}, bf16[8,16,512]{2,1,0:T(8,128)(2,1)S(1)}, u32[]{:S(2)}) copy-start(bf16[8,16,512]{2,1,0:T(8,128)(2,1)S(1)} %all-to-all-done.1.adjs) | copy-start | bytes 393220
  51.4 29.6 %all-to-all-start = ((bf16[8,512,128]{2,1,0:T(8,128)(2,1)}), bf16[8,512,128]{2,1,0:T(8,128)(2,1)S(1)}, u32[]{:S(2)}, u32[]{:S(2)}) async-start(bf16[8,512,128]{2,1,0:T(8,128)(2,1)} %get-tuple-element.13), calls=%async_computation | async-start | bytes 2097152 | tf_op jit(solution)/shard_map/all_to_all | solution.py:314
  59.0 1.0 copy-start.2
  66.1 2.9 %collective-permute-start.1 = (bf16[512,1024]{1,0:T(8,128)(2,1)}, bf16[512,1024]{1,0:T(8,128)(2,1)S(1)}, u32[]{:S(2)}, u32[]{:S(2)}) collective-permute-start(bf16[512,1024]{1,0:T(8,128)(2,1)} %shard_map.88.refs_1_), channel_id=1, source_target_pairs={{0,1},{1,0},{2,3},{3,2},{4,5},{5,4},{6,7},{7,6},{8,9},{9,8},{10,11... | collective-permute-start | bytes 3145736 | tf_op jit(solution)/shard_map/ppermute | solution.py:325
  68.9 1.0 copy-start.3
  81.0 1.0 copy-start
  89.4 11.0 %all-to-all-start.3 = ((bf16[8,16,512]{2,1,0:T(8,128)(2,1)}), bf16[8,16,512]{2,1,0:T(8,128)(2,1)S(1)}, u32[]{:S(2)}, u32[]{:S(2)}) async-start(bf16[8,16,512]{2,1,0:T(8,128)(2,1)} %get-tuple-element.17), calls=%async_computation.3 | async-start | bytes 262144 | tf_op jit(solution)/shard_map/all_to_all | solution.py:336
  100.4 28.5 %copy-start.4 = (bf16[8,16,512]{2,1,0:T(8,128)(2,1)}, bf16[8,16,512]{2,1,0:T(8,128)(2,1)S(1)}, u32[]{:S(2)}) copy-start(bf16[8,16,512]{2,1,0:T(8,128)(2,1)S(1)} %all-to-all-done.3.sides) | copy-start | bytes 393220
  100.4 28.5 %all-to-all-start.2 = ((bf16[8,512,128]{2,1,0:T(8,128)(2,1)}), bf16[8,512,128]{2,1,0:T(8,128)(2,1)S(1)}, u32[]{:S(2)}, u32[]{:S(2)}) async-start(bf16[8,512,128]{2,1,0:T(8,128)(2,1)} %get-tuple-element.16), calls=%async_computation.2 | async-start | bytes 2097152 | tf_op jit(solution)/shard_map/all_to_all | solution.py:335
  128.9 1.0 copy-start.1
  135.7 4.1 %collective-permute-start.4 = (bf16[4,16,1024]{2,1,0:T(8,128)(2,1)S(1)}, bf16[4,16,1024]{2,1,0:T(8,128)(2,1)S(1)}, u32[]{:S(2)}, u32[]{:S(2)}) collective-permute-start(bf16[4,16,1024]{2,1,0:T(8,128)(2,1)S(1)} %get-tuple-element.55), channel_id=1, source_target_pairs={{0,1},{2,3},{4,5},{6,7},{8,9},{10,11},{12,13},{14,15},{16,17},{18,... | collective-permute-start | bytes 393224 | tf_op jit(solution)/shard_map/ppermute | solution.py:343
  137.0 3.2 %collective-permute-start.5 = (bf16[4,16,1024]{2,1,0:T(8,128)(2,1)S(1)}, bf16[4,16,1024]{2,1,0:T(8,128)(2,1)S(1)}, u32[]{:S(2)}, u32[]{:S(2)}) collective-permute-start(bf16[4,16,1024]{2,1,0:T(8,128)(2,1)S(1)} %get-tuple-element.54), channel_id=1, source_target_pairs={{1,0},{3,2},{5,4},{7,6},{9,8},{11,10},{13,12},{15,14},{17,16},{19,... | collective-permute-start | bytes 393224 | tf_op jit(solution)/shard_map/ppermute | solution.py:344
  139.8 0.7 copy-start.8
  140.2 0.7 copy-start.9
where the time goes:
time: 150 us
  Pallas kernels  47.9 us (32%)
  waiting for transfers between devices  46.3 us (31%)
  starting transfers between devices  24.5 us (16%)
  other arithmetic  17.6 us (12%)
  local copies, waits for them, and re-layouts  12.3 us (8%)
    all_to_all x1, waiting for transfers between devices, per_device(): main = lax.all_to_all(ext, 'chan', 0, 0, tiled=True)  23.1 us
    pallas_call x1, Pallas kernels, per_device(): call(scall, [(NB, C, R, W)], [(NB, RP, C * W)])  8.7 us
    convert_element_type x1, other arithmetic, col_dft(): (-jnp.sin(phases) * factor).astype(bf16)  8.61 us
    all_to_all x1, waiting for transfers between devices, per_device(): adjs = lax.all_to_all(adjs, 'chan', 0, 0, tiled=True)  8.15 us
    pallas_call x1, Pallas kernels, per_device(): call(functools.partial(image_body, FC, FR, R, W), [(FC, FR * R, W), (C, R...  7.43 us
    all_to_all x1, starting transfers between devices, per_device(): adjs = lax.all_to_all(adjs, 'chan', 0, 0, tiled=True)  7.31 us
    all_to_all x1, waiting for transfers between devices, per_device(): sides = lax.all_to_all(exts, 'chan', 0, 0, tiled=True)  7.26 us
    pallas_call x1, Pallas kernels, per_device(): call(functools.partial(adjoint_body, C, R, W, B), [(C, R, W), (C, 16, R)]...  6.87 us
  transfers between devices with their start and end apart: 10, of which 6 were waited for; matrix products, arithmetic and copies ran while one was open for 9% of the time, Pallas kernels for 15%

commit v1 on v0

v1 whole, which is shorter than its diff:
```python
import functools
import math

import jax
import jax.numpy as jnp
import numpy as np
from jax import lax
from jax.experimental import pallas as pl
from jax.experimental.pallas import tpu as pltpu
from jax.sharding import PartitionSpec as P

NB = 4
TAPS = 17
MARGIN = 8
PAD = 16

primal_step = 0.5
dual_step = 0.5
radius = 6.0
weight_unit = 0.25
f32 = jnp.float32
bf16 = jnp.bfloat16


def dot(a, b):
    return jnp.dot(a, b, preferred_element_type=f32)


def col_dft(npix):
    half = npix // 2
    product = np.arange(npix)[:, None] * np.arange(half)[None, :] % npix
    phases = product.astype(np.float32) * np.float32(2.0 * math.pi / npix)
    factor = np.float32(1.0 / math.sqrt(npix))
    table = np.concatenate([np.cos(phases) * factor, -np.sin(phases) * factor], axis=1)
    return jnp.asarray(table.astype(jnp.bfloat16))


def side_cols(k, width):
    return jnp.where(k < MARGIN, k - MARGIN, width - MARGIN + k)


def toeplitz(taps, index):
    out = jnp.zeros((NB,) + index.shape, f32)
    for t in range(TAPS):
        out = jnp.where(index[None] == t, taps[:, t][:, None, None], out)
    return out


def adjoint_tables(row_taps, col_taps, width, block):
    h = row_taps.astype(bf16).astype(f32)
    g = col_taps.astype(bf16).astype(f32)
    i = jnp.arange(width)[:, None]
    j = jnp.arange(width)[None, :]
    main = toeplitz(g, j - i + MARGIN)
    k = jnp.arange(width)[None, :]
    side_index = jnp.where(k < 2 * MARGIN, side_cols(k, width) - i + MARGIN, -1)
    side = toeplitz(g, side_index)
    cols = jnp.concatenate([main, side], axis=2).astype(bf16)
    r = jnp.arange(block)[:, None]
    w = jnp.arange(NB * (block + 2 * PAD))[None, :]
    span = block + 2 * PAD
    rows = jnp.zeros((block, NB * span), f32)
    index = r - w % span + PAD + MARGIN
    for t in range(TAPS):
        tap_row = jnp.repeat(h[:, t], span)[None, :]
        rows = jnp.where(index == t, tap_row, rows)
    return cols, rows.astype(bf16)


def forward_tables(row_taps, col_taps, width, block):
    h = row_taps.astype(bf16).astype(f32)
    g = col_taps.astype(bf16).astype(f32)
    i = jnp.arange(width)[:, None]
    j = jnp.arange(NB * width)[None, :]
    main_index = i - j % width + MARGIN
    side_index = jnp.where(i < 2 * MARGIN, side_cols(i, width) - j % width + MARGIN, -1)
    index = jnp.concatenate([main_index, side_index], axis=0)
    cols = jnp.zeros(index.shape, f32)
    for t in range(TAPS):
        tap_row = jnp.repeat(g[:, t], width)[None, :]
        cols = jnp.where(index == t, tap_row, cols)
    r = jnp.arange(block)[:, None]
    w = jnp.arange(block + 2 * PAD)[None, :]
    rows = toeplitz(h, w - r - PAD + MARGIN)
    return cols.astype(bf16), rows.astype(bf16)


def spill_tables(fcols, width):
    span = 2 * MARGIN
    row = jnp.arange(fcols * span)[:, None]
    col = jnp.arange(fcols * width)[None, :]
    rb, rk = row // span, row % span
    gather = jnp.where(rk >= MARGIN, (rb + 1) * width + rk - MARGIN, rb * width - MARGIN + rk)
    table = (gather == col).astype(bf16)
    return table


def adjoint_group(R, W, B, first, channel, u, up, lo, gcols, hrows, adj, adjs, dc, dcs, main_done, side_done):
    per = W // 16
    span = B + 2 * PAD
    mains = [gcols[n, :, :W] for n in range(NB)]
    hr = hrows[...]
    for pair in range(0, per, 2):
        for n in range(NB):
            acc = None
            for e in range(2):
                c = channel(first + pair + e)
                shift = 16 * (pair + e)
                side = gcols[n, :, W:].astype(f32)
                side = pltpu.roll(side, shift, 1) if shift else side
                table = jnp.concatenate([mains[n], side.astype(bf16)], axis=1)
                rows = jnp.concatenate([up[n, c], u[n, c], lo[n, c]], axis=0)
                out = dot(rows, table)
                dc[n, :, e * W : (e + 1) * W] = out[:, :W].astype(bf16)
                acc = out[:, W:] if acc is None else acc + out[:, W:]
            if pair:
                dcs[n] = dcs[n] + acc.astype(bf16)
            else:
                dcs[n] = acc.astype(bf16)
        for k in range(R // B):
            win = jnp.concatenate([dc[n, k * B : k * B + span] for n in range(NB)], axis=0)
            out = dot(hr, win).astype(bf16)
            adj[first + pair, k * B : k * B + B] = out[:, :W]
            adj[first + pair + 1, k * B : k * B + B] = out[:, W:]
        main_done(first + pair)
        main_done(first + pair + 1)
    for k in range(R // B):
        win = jnp.concatenate([dcs[n, k * B : k * B + span] for n in range(NB)], axis=0)
        out = dot(hr, win).T.astype(bf16)
        for cc in range(per):
            adjs[first + cc, :, k * B : k * B + B] = out[cc * 16 : cc * 16 + 16]
    for cc in range(per):
        side_done(first + cc)


def half_body(FC, W, x, colT, out):
    full = out.shape[1]
    rows = jnp.concatenate([x[b] for b in range(FC)], axis=1)

    @pl.loop(0, full // 256)
    def _(j):
        lanes = pl.ds(pl.multiple_of(j * 256, 256), 256)
        out[:, lanes] = dot(rows, colT[:, lanes]).astype(bf16)


def table_body(s, FR, R, colT, bown, aown, aoth):
    half = FR * R
    for a in range(FR):
        own = pl.ds(pl.multiple_of((2 * a + s) * R, R), R)
        bown[a * R : (a + 1) * R] = colT[own, :]
    sign_row = lax.broadcasted_iota(jnp.int32, (1, half), 1) % 2
    flip = jnp.where((sign_row == 1) & (s == 1), -1.0, 1.0).astype(f32)
    for dst, part in ((aown, s), (aoth, 1 - s)):
        for q in range(2):
            pieces = [
                colT[pl.ds(pl.multiple_of((2 * a + part) * R, R), R), q * half : (q + 1) * half]
                for a in range(FR)
            ]
            block = jnp.concatenate(pieces, axis=0) if FR > 1 else pieces[0]
            dst[:, q * half : (q + 1) * half] = (block.astype(f32).T * flip).astype(bf16)


def stack_re_im(ref, lanes_re, lanes_im, transpose):
    re, im = ref[:, lanes_re], ref[:, lanes_im]
    if transpose:
        return jnp.concatenate([re, im], 0), jnp.concatenate([im, -re], 0)
    return jnp.concatenate([re, -im], 0), jnp.concatenate([im, re], 0)


def vis_body(half, aown, aoth, hown, hoth, wts, out):
    step = 256

    @pl.loop(0, half // step)
    def _(j):
        re_l = pl.ds(pl.multiple_of(j * step, step), step)
        im_l = pl.ds(pl.multiple_of(j * step + half, step), step)
        own_re, own_im = stack_re_im(hown, re_l, im_l, False)
        oth_re, oth_im = stack_re_im(hoth, re_l, im_l, False)
        scale = weight_unit * wts[:, re_l].astype(f32)
        re = dot(aown[...], own_re) + dot(aoth[...], oth_re)
        out[:, re_l] = (scale * re).astype(bf16)
        im = dot(aown[...], own_im) + dot(aoth[...], oth_im)
        out[:, im_l] = (scale * im).astype(bf16)


def back_body(s, half, bown, wown, woth, out):
    step = 256
    odd = lax.broadcasted_iota(jnp.int32, (half, 1), 0) % 2 == 1
    own_sign = jnp.where(odd & (s == 1), -1.0, 1.0)
    oth_sign = jnp.where(odd & (s == 0), -1.0, 1.0)

    @pl.loop(0, half // step)
    def _(j):
        re_l = pl.ds(pl.multiple_of(j * step, step), step)
        im_l = pl.ds(pl.multiple_of(j * step + half, step), step)
        own_re, own_im = stack_re_im(wown, re_l, im_l, True)
        oth_re, oth_im = stack_re_im(woth, re_l, im_l, True)
        re = own_sign * dot(bown[...], own_re) + oth_sign * dot(bown[...], oth_re)
        out[:, re_l] = re.astype(bf16)
        im = own_sign * dot(bown[...], own_im) + oth_sign * dot(bown[...], oth_im)
        out[:, im_l] = im.astype(bf16)


def gradient_body(FC, W, back, colT, x, d, pre):
    step = 2 * W

    @pl.loop(0, FC // 2)
    def _(j):
        lanes = pl.ds(pl.multiple_of(j * step, step), step)
        grad = lax.dot_general(
            back[...], colT[lanes, :], (((1,), (1,)), ((), ())), preferred_element_type=f32
        )
        xs = jnp.concatenate([x[2 * j], x[2 * j + 1]], axis=1).astype(f32)
        ds = jnp.concatenate([d[2 * j], d[2 * j + 1]], axis=1).astype(f32)
        pre[:, lanes] = xs - primal_step * (grad - ds)


def side_rows(FC, FR, adjs):
    st_rows = []
    for a in range(FR):
        parts = jnp.concatenate([adjs[b * FR + a] for b in range(FC)], axis=0)
        st_rows.append(parts.astype(f32).T.astype(bf16))
    return jnp.concatenate(st_rows, axis=0) if FR > 1 else st_rows[0]


def forward_cols_body(C, R, W, main, sides, fcols, ic):
    per = W // 16
    for c0 in range(0, C, per):
        parts = jnp.concatenate([sides[c0 + cc] for cc in range(per)], axis=0)
        st = parts.astype(f32).T.astype(bf16)
        for cc in range(per):
            c = c0 + cc
            zeros_a = jnp.zeros((cc * 16, NB * W), bf16)
            zeros_b = jnp.zeros((W - 16 - cc * 16, NB * W), bf16)
            pieces = [fcols[:W], fcols[W : W + 16]]
            if cc:
                pieces.insert(1, zeros_a)
            if cc < per - 1:
                pieces.append(zeros_b)
            table = jnp.concatenate(pieces, axis=0)
            out = dot(jnp.concatenate([main[c], st], axis=1), table)
            for n in range(NB):
                ic[n, PAD : PAD + R, c * W : (c + 1) * W] = out[:, n * W : (n + 1) * W].astype(bf16)


def shrink_body(C, R, W, B, ic, frows, u, mask, new_in, out, new_out):
    span = B + 2 * PAD
    new_out[...] = new_in[...]
    hr = frows[0]
    for k in range(R // B):
        rows = slice(k * B, (k + 1) * B)
        keep = radius * mask[rows].astype(f32)
        coef = dot(hr, ic[0, k * B : k * B + span])
        total = None
        steps = []
        for c in range(C):
            st = u[0, c, rows].astype(f32) + dual_step * coef[:, c * W : (c + 1) * W]
            steps.append(st)
            total = st * st if total is None else total + st * st
        scale = keep / jnp.maximum(jnp.sqrt(total), radius)
        for c in range(C):
            out[0, c, rows] = (steps[c] * scale).astype(bf16)


def step_kernel(
    C, FC, FR, R, W, B,
    u, x, d, wts, colT, spill, gcols, hrows, fcols,
    new, ic,
    up, lo, dc, dcs, adj, adjs, radj, radjs,
    hown, hoth, wown, woth, back, bown, aown, aoth, pre,
    ext, exts, rmain, rsides, htop, hbot,
    send_u, recv_u, send_a, recv_a, send_as, recv_as,
    send_e, recv_e, send_es, recv_es, send_p, recv_p, send_h, recv_h,
):
    half = FC * W // 2
    me = lax.axis_index("chan")
    s = lax.axis_index("split")
    ma, mb = me % FR, me // FR
    has_up = (ma > 0) | (s == 1)
    has_down = (ma < FR - 1) | (s == 0)
    partner = {"chan": me, "split": 1 - s}
    down_id = {"chan": (me + s) % C, "split": 1 - s}
    up_id = {"chan": (me + s + C - 1) % C, "split": 1 - s}
    per = W // 16

    def remote(src, dst, ssem, rsem, device):
        return pltpu.make_async_remote_copy(
            src_ref=src, dst_ref=dst, send_sem=ssem, recv_sem=rsem,
            device_id=device, device_id_type=pl.DeviceIdType.MESH,
        )

    barrier = pltpu.get_barrier_semaphore()

    @pl.loop(1, C)
    def _(i):
        pl.semaphore_signal(
            barrier, inc=1, device_id={"chan": (me + i) % C, "split": s},
            device_id_type=pl.DeviceIdType.MESH,
        )

    pl.semaphore_signal(barrier, inc=1, device_id=partner, device_id_type=pl.DeviceIdType.MESH)
    if FR > 1:
        cross = jnp.where(s == 0, ma > 0, ma < FR - 1)
        cross_chan = jnp.where(s == 0, (me + C - 1) % C, (me + 1) % C)

        @pl.when(cross)
        def _():
            pl.semaphore_signal(
                barrier, inc=1, device_id={"chan": cross_chan, "split": 1 - s},
                device_id_type=pl.DeviceIdType.MESH,
            )
            pl.semaphore_wait(barrier, 1)

    pl.semaphore_wait(barrier, C)

    def chain(down_src, down_dst, up_src, up_dst, ssem, rsem):
        downward = remote(down_src, down_dst, ssem.at[0], rsem.at[0], down_id)
        upward = remote(up_src, up_dst, ssem.at[1], rsem.at[1], up_id)

        @pl.when(has_down)
        def _():
            downward.start()

        @pl.when(has_up)
        def _():
            upward.start()

        @pl.when(jnp.logical_not(has_up))
        def _():
            down_dst[...] = jnp.zeros_like(down_dst)

        @pl.when(jnp.logical_not(has_down))
        def _():
            up_dst[...] = jnp.zeros_like(up_dst)

        def finish():
            @pl.when(has_down)
            def _():
                downward.wait_send()
                upward.wait_recv()

            @pl.when(has_up)
            def _():
                upward.wait_send()
                downward.wait_recv()

        return finish

    finish_u = chain(u.at[:, :, pl.ds(R - PAD, PAD)], up, u.at[:, :, pl.ds(0, PAD)], lo, send_u, recv_u)
    table_body(s, FR, R, colT, bown, aown, aoth)
    finish_u()

    def peer(i):
        return (me + 1 + i) % C

    def send(buf, dst, ssem, rsem):
        def start(i):
            @pl.when(i < C - 1)
            def _():
                remote(
                    buf.at[i], dst.at[me], ssem.at[i], rsem.at[i], {"chan": peer(i), "split": s}
                ).start()

            @pl.when(i == C - 1)
            def _():
                dst[me] = buf[i]

        return start

    def finish(buf, dst, ssem, rsem):
        @pl.loop(0, C - 1)
        def _(i):
            remote(
                buf.at[i], dst.at[me], ssem.at[i], rsem.at[i], {"chan": peer(i), "split": s}
            ).wait()

    @pl.loop(0, C // per)
    def _(g):
        adjoint_group(
            R, W, B, g * per, peer, u, up, lo, gcols, hrows, adj, adjs, dc, dcs,
            send(adj, radj, send_a, recv_a), send(adjs, radjs, send_as, recv_as),
        )

    half_body(FC, W, x, colT, hown)
    copy = remote(hown, hoth, send_p.at[0], recv_p.at[0], partner)
    copy.start()
    copy.wait()
    vis_body(half, aown, aoth, hown, hoth, wts, wown)
    copy = remote(wown, woth, send_p.at[1], recv_p.at[1], partner)
    copy.start()
    copy.wait()
    back_body(s, half, bown, wown, woth, back)
    gradient_body(FC, W, back, colT, x, d, pre)

    finish(adjs, radjs, send_as, recv_as)
    finish(adj, radj, send_a, recv_a)
    st = side_rows(FC, FR, radjs)
    es = None
    for i in range(FC):
        b = (mb + 1 + i) % FC
        lanes = pl.ds(pl.multiple_of(b * W, W), W)
        table = spill[:, lanes]
        pieces = [radj[b * FR + a] for a in range(FR)]
        main = jnp.concatenate(pieces, axis=0) if FR > 1 else pieces[0]
        upd = pre[:, lanes] - primal_step * (main.astype(f32) + dot(st, table))
        nb = jnp.maximum(upd, 0.0).astype(bf16)
        eb = (2.0 * nb.astype(f32) - x[b].astype(f32)).astype(bf16)
        new[b] = nb
        for a in range(FR):
            ext[b * FR + a] = eb[a * R : (a + 1) * R]
        part = lax.dot_general(eb, table, (((1,), (1,)), ((), ())), preferred_element_type=f32)
        es = part if es is None else es + part
        for j in range(FR):
            f = b * FR + (ma + j) % FR
            r = i * FR + j
            if i == FC - 1 and j == 0:
                rmain[me] = eb if FR == 1 else ext[f]
            else:
                remote(
                    ext.at[f], rmain.at[me], send_e.at[r], recv_e.at[r], {"chan": f, "split": s}
                ).start()
    for a in range(FR):
        t = es[a * R : (a + 1) * R].T.astype(bf16)
        for b in range(FC):
            exts[b * FR + a] = t[b * 16 : b * 16 + 16]
    sides = []
    for i in range(FC):
        for j in range(FR):
            f = (mb + 1 + i) % FC * FR + (ma + j) % FR
            r = i * FR + j
            if i == FC - 1 and j == 0:
                rsides[me] = exts[f]
            else:
                remote(
                    exts.at[f], rsides.at[me], send_es.at[r], recv_es.at[r],
                    {"chan": f, "split": s},
                ).start()
    for i in range(FC):
        for j in range(FR):
            f = (mb + 1 + i) % FC * FR + (ma + j) % FR
            r = i * FR + j
            if i == FC - 1 and j == 0:
                continue
            device = {"chan": f, "split": s}
            remote(exts.at[f], rsides.at[me], send_es.at[r], recv_es.at[r], device).wait()
            remote(ext.at[f], rmain.at[me], send_e.at[r], recv_e.at[r], device).wait()
    forward_cols_body(C, R, W, rmain, rsides, fcols, ic)
    finish_h = chain(
        ic.at[:, pl.ds(R, PAD)], htop, ic.at[:, pl.ds(PAD, PAD)], hbot, send_h, recv_h
    )
    finish_h()
    ic[:, :PAD] = htop[...]
    ic[:, PAD + R :] = hbot[...]


def per_device(sky_image, dirty_image, uv_weights, dual_coeffs, support_mask, row_taps, col_taps):
    FC, FR = sky_image.shape[1], sky_image.shape[2]
    R, W = sky_image.shape[4], sky_image.shape[5]
    C = dual_coeffs.shape[1]
    npix = FC * W
    half = npix // 2
    B = min(128, R)
    RP = R + 2 * PAD
    u = dual_coeffs.reshape(NB, C, R, W)
    x = sky_image.reshape(FC, FR * R, W)
    d = dirty_image.reshape(FC, FR * R, W)
    wts = uv_weights.reshape(half, half)
    mask = support_mask.reshape(R, W)
    colT = col_dft(npix)
    spill = spill_tables(FC, W)
    gcols, hrows = adjoint_tables(row_taps, col_taps, W, B)
    fcols, frows = forward_tables(row_taps, col_taps, W, B)
    vm = lambda *shape: pltpu.VMEM(shape, bf16)
    sem = lambda n: pltpu.SemaphoreType.DMA((n,))
    new, ic = pl.pallas_call(
        functools.partial(step_kernel, C, FC, FR, R, W, B),
        out_shape=[
            jax.ShapeDtypeStruct((FC, FR * R, W), bf16),
            jax.ShapeDtypeStruct((NB, RP, C * W), bf16),
        ],
        scratch_shapes=[
            vm(NB, C, PAD, W), vm(NB, C, PAD, W), vm(NB, RP, 2 * W), vm(NB, RP, W),
            vm(C, R, W), vm(C, 16, R), vm(C, R, W), vm(C, 16, R),
            *[vm(half, npix)] * 8, pltpu.VMEM((half, npix), f32),
            vm(C, R, W), vm(C, 16, R), vm(C, R, W), vm(C, 16, R),
            vm(NB, PAD, C * W), vm(NB, PAD, C * W),
            sem(2), sem(2), sem(C), sem(C), sem(C), sem(C),
            sem(C), sem(C), sem(C), sem(C), sem(2), sem(2), sem(2), sem(2),
        ],
        compiler_params=pltpu.CompilerParams(
            collective_id=0, has_side_effects=True, vmem_limit_bytes=58 * 2**20
        ),
    )(u, x, d, wts, colT, spill, gcols, hrows, fcols)

    part = FC // NB
    new_dual, new = pl.pallas_call(
        functools.partial(shrink_body, C, R, W, B),
        grid=(NB,),
        in_specs=[
            pl.BlockSpec((1, RP, C * W), lambda n: (n, 0, 0)),
            pl.BlockSpec((1, B, B + 2 * PAD), lambda n: (n, 0, 0)),
            pl.BlockSpec((1, C, R, W), lambda n: (n, 0, 0, 0)),
            pl.BlockSpec((R, W), lambda n: (0, 0)),
            pl.BlockSpec((part, FR * R, W), lambda n: (n, 0, 0)),
        ],
        out_specs=[
            pl.BlockSpec((1, C, R, W), lambda n: (n, 0, 0, 0)),
            pl.BlockSpec((part, FR * R, W), lambda n: (n, 0, 0)),
        ],
        out_shape=[
            jax.ShapeDtypeStruct((NB, C, R, W), bf16),
            jax.ShapeDtypeStruct((FC, FR * R, W), bf16),
        ],
    )(ic, frows, u, mask, new)
    return (new.reshape(sky_image.shape), new_dual.reshape(dual_coeffs.shape))


def solution(mesh):
    placed = (
        P(("cube", "chan"), None, None, "split", None, None),
        P(("cube", "chan"), None, None, "split", None, None),
        P(("cube", "chan"), "split", None),
        P(None, "cube", "chan", "split", None, None),
        P("chan", "split", None, None),
        P(),
        P(),
    )
    return jax.shard_map(
        per_device,
        mesh=mesh,
        in_specs=placed,
        out_specs=(
            P(("cube", "chan"), None, None, "split", None, None),
            P(None, "cube", "chan", "split", None, None),
        ),
        check_vma=False,
    )
```

time: 150 us -> 94.4 us (0.63)
  waiting for transfers between devices: 46.3 us -> 0 us
  Pallas kernels: 47.9 us -> 80.2 us
  starting transfers between devices: 24.5 us -> 0 us
  other arithmetic: 17.6 us -> 8.81 us
  local copies, waits for them, and re-layouts: 12.3 us -> 4.4 us
    all_to_all x4 -> x0, waiting for transfers between devices: 44.1 us -> none  [the longest x1 23.1 us: per_device(): main = lax.all_to_all(ext, 'chan', 0, 0, tiled=True)]
    pallas_call x8 -> x2, Pallas kernels: 47.9 us -> 80.2 us  [the longest x1 72.2 us: per_device(): pl.pallas_call(functools.partial(step_kernel, C, FC, FR, R, W, B), out_sh...]
    all_to_all x4 -> x0, starting transfers between devices: 18.2 us -> none  [the longest x1 7.31 us: per_device(): adjs = lax.all_to_all(adjs, 'chan', 0, 0, tiled=True)]
    convert_element_type x1 -> x0, other arithmetic: 8.61 us -> none  [col_dft(): (-jnp.sin(phases) * factor).astype(bf16)]
    ppermute x6 -> x0, starting transfers between devices: 6.31 us -> none  [the longest x1 1.93 us: per_device(): up = lax.ppermute(u[:, :, R - PAD:], chain, down)]
    unnamed x24 -> x0, local copies, waits for them, and re-layouts: 5.91 us -> none
    ppermute x6 -> x0, waiting for transfers between devices: 2.28 us -> none  [the longest x1 1.8 us: per_device(): woth = lax.ppermute(wown, 'split', swap)]
    slice x2 -> x0, local copies, waits for them, and re-layouts: 1.98 us -> none  [the longest x1 0.99 us: per_device(): lo = lax.ppermute(u[:, :, :PAD], chain, upward)]
  transfers between devices with their start and end apart: 10 -> 0, of which waited for: 6 -> 0; matrix products, arithmetic and copies ran while one was open for 9% -> 0% of each run, Pallas kernels for 15% -> 0%
where the time goes in v1:
time: 94.4 us; the launch traced here: 94.2 us
  Pallas kernels  80.2 us (85%)
  other arithmetic  8.81 us (9%)
  local copies, waits for them, and re-layouts  4.4 us (5%)
    pallas_call x1, Pallas kernels, per_device(): pl.pallas_call(functools.partial(step_kernel, C, FC, FR, R, W, B), out_sh...  72.2 us
    pallas_call x1, Pallas kernels, per_device(): pl.pallas_call(functools.partial(shrink_body, C, R, W, B), grid=(NB,), in...  8.03 us
    convert_element_type x2, other arithmetic, forward_tables(): return (cols.astype(bf16), rows.astype(bf16))  2.79 us

profile of v1, /device:TPU:0, one launch (start us, length us, event | category | flops | bytes accessed | tf_op | source)
XLA Modules:
  0.0 94.2 jit_solution(8225538764611537646)
XLA Ops:
  0.7 0.7 convert_convert_fusion
  1.4 0.7 convert_convert_fusion.1
  2.0 0.5 slice_reduce_fusion.33
  2.5 0.1 broadcast_bitcast_fusion.16
  2.6 0.1 broadcast_bitcast_fusion
  2.7 0.1 broadcast_bitcast_fusion.2
  2.7 0.1 broadcast_bitcast_fusion.4
  2.8 0.1 broadcast_bitcast_fusion.6
  2.9 0.1 broadcast_bitcast_fusion.8
  3.0 0.1 broadcast_bitcast_fusion.10
  3.0 0.1 broadcast_bitcast_fusion.12
  3.1 0.1 broadcast_bitcast_fusion.14
  3.2 0.5 slice_reduce_fusion.16
  3.7 0.1 broadcast_in_dim.1065
  3.7 0.1 broadcast_in_dim.1066
  3.8 0.1 broadcast_in_dim.1113
  3.9 0.1 broadcast_in_dim.1114
  4.0 0.1 broadcast_in_dim.1110
  4.1 0.1 broadcast_in_dim.1111
  4.2 0.1 broadcast_in_dim.1107
  4.2 0.1 broadcast_in_dim.1108
  4.3 0.1 broadcast_in_dim.1104
  4.4 0.1 broadcast_in_dim.1105
  4.5 0.1 broadcast_in_dim.1101
  4.6 0.1 broadcast_in_dim.1102
  4.7 0.1 broadcast_in_dim.1099
  4.8 0.1 broadcast_in_dim.1095
  4.9 0.1 broadcast_in_dim.1096
  5.1 0.1 broadcast_in_dim.1093
  5.2 0.1 broadcast_in_dim.1090
  5.4 0.1 broadcast_in_dim.1087
  5.5 0.1 broadcast_in_dim.1084
  5.7 0.1 broadcast_in_dim.1081
  5.9 0.1 broadcast_in_dim.1078
  6.0 0.1 broadcast_in_dim.1075
  6.2 0.1 broadcast_in_dim.1072
  6.4 0.1 broadcast_in_dim.1069
  6.8 0.6 select_convert_fusion.4
  7.7 1.5 %select_convert_fusion.frows = bf16[4,128,160]{2,1,0:T(8,128)(2,1)} fusion(bf16[4]{0:T(256)(128)(2,1)S(1)} %get-tuple-element.13, bf16[4]{0:T(256)(128)(2,1)S(1)} %get-tuple-element.14, bf16[4]{0:T(256)(128)(2,1)S(1)} %get-tuple-element.15, bf16[4]{0:T(256)(128)(2,1)S(1)} %get-tuple-element.16, bf16[4]{0:T(256)(128)(2,1)S(1)} %get-tuple-element.17, ...), kind=kLoop, calls=%fused_computation.1 | loop fusion | flops 1392640 | bytes 512136 | tf_op jit(solution)/shard_map/convert_element_type | solution.py:85
  9.2 1.1 %select_convert_fusion.2.hrows = bf16[128,640]{1,0:T(8,128)(2,1)} fusion(bf16[640]{0:T(1024)(128)(2,1)S(1)} %broadcast_in_dim.1114, bf16[640]{0:T(1024)(128)(2,1)S(1)} %broadcast_in_dim.1111, bf16[640]{0:T(1024)(128)(2,1)S(1)} %broadcast_in_dim.1108, bf16[640]{0:T(1024)(128)(2,1)S(1)} %broadcast_in_dim.1105, bf16[640]{0:T(1024)(128)(2,1)S(1)} %broadcast_in_dim.1102, ...), kind=kLoop, calls=%fused_computation.5 | loop fusion | flops 2949120 | bytes 188160 | tf_op jit(solution)/shard_map/convert_element_type | solution.py:67
  10.3 0.8 fusion.spill
  11.1 0.2 fusion.51
  11.3 0.6 select_convert_fusion.3
  11.9 0.7 pad_maximum_fusion.gcols
  12.6 0.1 subtract_add_fusion.1
  12.7 1.3 %select_convert_fusion.1.fcols = bf16[256,512]{1,0:T(8,128)(2,1)} fusion(s32[128,512]{1,0:T(8,128)S(1)} %get-tuple-element.47, s32[128,512]{1,0:T(8,128)S(1)} %get-tuple-element.46, bf16[512]{0:T(512)(128)(2,1)S(1)} %get-tuple-element.65, bf16[512]{0:T(512)(128)(2,1)S(1)} %get-tuple-element.66, bf16[512]{0:T(512)(128)(2,1)S(1)} %get-tuple-element.67, ...), kind=kLoop, calls=%fused_computation.2 | loop fusion | flops 4587520 | bytes 803840 | tf_op jit(solution)/shard_map/convert_element_type | solution.py:85
  14.0 72.2 %shard_map.95 = (bf16[8,512,128]{2,1,0:T(8,128)(2,1)}, bf16[4,544,1024]{2,1,0:T(8,128)(2,1)}) custom-call(bf16[4,8,512,128]{3,2,1,0:T(8,128)(2,1)} %bitcast.45, bf16[8,512,128]{2,1,0:T(8,128)(2,1)} %bitcast.47, bf16[8,512,128]{2,1,0:T(8,128)(2,1)} %bitcast.48, s32[512,512]{1,0:T(8,128)} %bitcast.49, bf16[1024,1024]{1,0:T(8,128)(2,1)} %constant.70.clone.colT, ...), custom_call_target="tpu_custom_call" | custom-call | tf_op jit(solution)/shard_map/pallas_call | solution.py:475
  86.2 8.0 %shard_map.96 = (bf16[4,8,512,128]{3,2,1,0:T(8,128)(2,1)}, bf16[8,512,128]{2,1,0:T(8,128)(2,1)}) custom-call(bf16[4,544,1024]{2,1,0:T(8,128)(2,1)} %get-tuple-element.6.ic, bf16[4,128,160]{2,1,0:T(8,128)(2,1)} %select_convert_fusion.frows, bf16[4,8,512,128]{3,2,1,0:T(8,128)(2,1)} %bitcast.46, s32[512,128]{1,0:T(8,128)} %bitcast.50, ...), custom_call_target="tpu_custom_call" | custom-call | tf_op jit(solution)/shard_map/pallas_call | solution.py:496
  (33 shorter events, 1.3 us)

commit v2 on v1

v2 whole, which is shorter than its diff:
```python
import functools
import math

import jax
import jax.numpy as jnp
import numpy as np
from jax import lax
from jax.experimental import pallas as pl
from jax.experimental.pallas import tpu as pltpu
from jax.sharding import PartitionSpec as P

NB = 4
TAPS = 17
MARGIN = 8
PAD = 16

primal_step = 0.5
dual_step = 0.5
radius = 6.0
weight_unit = 0.25
f32 = jnp.float32
bf16 = jnp.bfloat16


def dot(a, b):
    return jnp.dot(a, b, preferred_element_type=f32)


def col_dft(npix):
    half = npix // 2
    product = np.arange(npix)[:, None] * np.arange(half)[None, :] % npix
    phases = product.astype(np.float32) * np.float32(2.0 * math.pi / npix)
    factor = np.float32(1.0 / math.sqrt(npix))
    table = np.concatenate([np.cos(phases) * factor, -np.sin(phases) * factor], axis=1)
    return jnp.asarray(table.astype(jnp.bfloat16))


def bands(index, taps):
    outs = [jnp.zeros(index.shape, f32) for _ in range(NB)]
    for t in range(TAPS):
        hit = index == t
        outs = [jnp.where(hit, taps[n, t], outs[n]) for n in range(NB)]
    return [o.astype(bf16) for o in outs]


def adjoint_tables(W, B, row_taps, col_taps, gcols, hrows):
    i = lax.broadcasted_iota(jnp.int32, (W, W), 0)
    j = lax.broadcasted_iota(jnp.int32, (W, W), 1)
    side = jnp.where(j < MARGIN, j - MARGIN, W - MARGIN + j)
    main_bands = bands(j - i + MARGIN, col_taps)
    side_bands = bands(jnp.where(j < 2 * MARGIN, side - i + MARGIN, -1), col_taps)
    r = lax.broadcasted_iota(jnp.int32, (B, B + 2 * PAD), 0)
    w = lax.broadcasted_iota(jnp.int32, (B, B + 2 * PAD), 1)
    row_bands = bands(r - w + PAD + MARGIN, row_taps)
    for n in range(NB):
        gcols[n, :, :W] = main_bands[n]
        gcols[n, :, W:] = side_bands[n]
        hrows[n] = row_bands[n]


def forward_tables(W, B, row_taps, col_taps, fcols, frows):
    i = lax.broadcasted_iota(jnp.int32, (W, W), 0)
    j = lax.broadcasted_iota(jnp.int32, (W, W), 1)
    main_bands = bands(i - j + MARGIN, col_taps)
    k = lax.broadcasted_iota(jnp.int32, (2 * MARGIN, W), 0)
    jk = lax.broadcasted_iota(jnp.int32, (2 * MARGIN, W), 1)
    side = jnp.where(k < MARGIN, k - MARGIN, W - MARGIN + k)
    side_bands = bands(side - jk + MARGIN, col_taps)
    r = lax.broadcasted_iota(jnp.int32, (B, B + 2 * PAD), 0)
    w = lax.broadcasted_iota(jnp.int32, (B, B + 2 * PAD), 1)
    row_bands = bands(w - r - PAD + MARGIN, row_taps)
    for n in range(NB):
        fcols[:W, n * W : (n + 1) * W] = main_bands[n]
        fcols[W:, n * W : (n + 1) * W] = side_bands[n]
        frows[n] = row_bands[n]


def spill_table(FC, W, spill):
    span = 2 * MARGIN
    row = lax.broadcasted_iota(jnp.int32, (FC * span, FC * W), 0)
    col = lax.broadcasted_iota(jnp.int32, (FC * span, FC * W), 1)
    rb, rk = row // span, row % span
    target = jnp.where(rk >= MARGIN, (rb + 1) * W + rk - MARGIN, rb * W - MARGIN + rk)
    spill[...] = jnp.where(target == col, 1.0, 0.0).astype(bf16)


def adjoint_group(R, W, B, first, channel, u, up, lo, gcols, hrows, adj, adjs, dc, dcs, main_done, side_done):
    per = W // 16
    span = B + 2 * PAD
    mains = [gcols[n, :, :W] for n in range(NB)]
    for pair in range(0, per, 2):
        for n in range(NB):
            acc = None
            for e in range(2):
                c = channel(first + pair + e)
                shift = 16 * (pair + e)
                side = gcols[n, :, W:].astype(f32)
                side = pltpu.roll(side, shift, 1) if shift else side
                table = jnp.concatenate([mains[n], side.astype(bf16)], axis=1)
                rows = jnp.concatenate([up[n, c], u[n, c], lo[n, c]], axis=0)
                out = dot(rows, table)
                dc[n, :, e * W : (e + 1) * W] = out[:, :W].astype(bf16)
                acc = out[:, W:] if acc is None else acc + out[:, W:]
            if pair:
                dcs[n] = dcs[n] + acc.astype(bf16)
            else:
                dcs[n] = acc.astype(bf16)
        for k in range(R // B):
            out = sum(dot(hrows[n], dc[n, k * B : k * B + span]) for n in range(NB)).astype(bf16)
            adj[first + pair, k * B : k * B + B] = out[:, :W]
            adj[first + pair + 1, k * B : k * B + B] = out[:, W:]
        main_done(first + pair)
        main_done(first + pair + 1)
    for k in range(R // B):
        out = sum(dot(hrows[n], dcs[n, k * B : k * B + span]) for n in range(NB)).T.astype(bf16)
        for cc in range(per):
            adjs[first + cc, :, k * B : k * B + B] = out[cc * 16 : cc * 16 + 16]
    for cc in range(per):
        side_done(first + cc)


def half_chunk(FC, x, colT, out, lanes):
    rows = jnp.concatenate([x[b] for b in range(FC)], axis=1)
    out[:, lanes] = dot(rows, colT[:, lanes]).astype(bf16)


def table_body(s, FR, R, colT, bown, aown, aoth):
    half = FR * R
    for a in range(FR):
        own = pl.ds(pl.multiple_of((2 * a + s) * R, R), R)
        bown[a * R : (a + 1) * R] = colT[own, :]
    odd_lane = lax.broadcasted_iota(jnp.int32, (1, half), 1) % 2 == 1
    flip = jnp.where(odd_lane & (s == 1), -1.0, 1.0).astype(f32)
    odd_row = lax.broadcasted_iota(jnp.int32, (half, 1), 0) % 2 == 1
    for dst, part in ((aown, s), (aoth, 1 - s)):
        for q in range(2):
            lanes = slice(q * half, (q + 1) * half)
            if FR == 1:
                sign = jnp.where(odd_row & (part == 1), -1.0, 1.0).astype(f32)
                dst[:, lanes] = (colT[:half, lanes].astype(f32) * (sign * flip)).astype(bf16)
                continue
            pieces = [
                colT[pl.ds(pl.multiple_of((2 * a + part) * R, R), R), lanes] for a in range(FR)
            ]
            block = jnp.concatenate(pieces, axis=0)
            dst[:, lanes] = (block.astype(f32).T * flip).astype(bf16)


def stack_re_im(ref, lanes_re, lanes_im, transpose):
    re, im = ref[:, lanes_re], ref[:, lanes_im]
    if transpose:
        return jnp.concatenate([re, im], 0), jnp.concatenate([im, -re], 0)
    return jnp.concatenate([re, -im], 0), jnp.concatenate([im, re], 0)


def vis_chunk(aown, aoth, hown, hoth, wts, out, re_l, im_l):
    own_re, own_im = stack_re_im(hown, re_l, im_l, False)
    oth_re, oth_im = stack_re_im(hoth, re_l, im_l, False)
    scale = weight_unit * wts[:, re_l].astype(f32)
    re = dot(aown[...], own_re) + dot(aoth[...], oth_re)
    out[:, re_l] = (scale * re).astype(bf16)
    im = dot(aown[...], own_im) + dot(aoth[...], oth_im)
    out[:, im_l] = (scale * im).astype(bf16)


def back_chunk(s, half, bown, wown, woth, out, re_l, im_l):
    odd = lax.broadcasted_iota(jnp.int32, (half, 1), 0) % 2 == 1
    own_sign = jnp.where(odd & (s == 1), -1.0, 1.0)
    oth_sign = jnp.where(odd & (s == 0), -1.0, 1.0)
    own_re, own_im = stack_re_im(wown, re_l, im_l, True)
    oth_re, oth_im = stack_re_im(woth, re_l, im_l, True)
    re = own_sign * dot(bown[...], own_re) + oth_sign * dot(bown[...], oth_re)
    out[:, re_l] = re.astype(bf16)
    im = own_sign * dot(bown[...], own_im) + oth_sign * dot(bown[...], oth_im)
    out[:, im_l] = im.astype(bf16)


def gradient_body(FC, W, back, colT, x, d, pre):
    step = 2 * W

    @pl.loop(0, FC // 2)
    def _(j):
        lanes = pl.ds(pl.multiple_of(j * step, step), step)
        grad = lax.dot_general(
            back[...], colT[lanes, :], (((1,), (1,)), ((), ())), preferred_element_type=f32
        )
        xs = jnp.concatenate([x[2 * j], x[2 * j + 1]], axis=1).astype(f32)
        ds = jnp.concatenate([d[2 * j], d[2 * j + 1]], axis=1).astype(f32)
        pre[:, lanes] = xs - primal_step * (grad - ds)


def side_rows(FC, FR, adjs):
    st_rows = []
    for a in range(FR):
        parts = jnp.concatenate([adjs[b * FR + a] for b in range(FC)], axis=0)
        st_rows.append(parts.astype(f32).T.astype(bf16))
    return jnp.concatenate(st_rows, axis=0) if FR > 1 else st_rows[0]


def forward_cols(R, W, c, main, sides, fcols, ic):
    out = dot(main[c], fcols[:W]) + lax.dot_general(
        sides[c], fcols[W:], (((0,), (0,)), ((), ())), preferred_element_type=f32
    )
    lanes = pl.ds(pl.multiple_of(c * W, W), W)
    for n in range(NB):
        ic[n, PAD : PAD + R, lanes] = out[:, n * W : (n + 1) * W].astype(bf16)


def shrink_body(C, R, W, B, ic, frows, u, mask, new_in, out, new_out):
    span = B + 2 * PAD
    new_out[...] = new_in[...]
    hr = frows[0]
    for k in range(R // B):
        rows = slice(k * B, (k + 1) * B)
        keep = radius * mask[rows].astype(f32)
        coef = dot(hr, ic[0, k * B : k * B + span])
        total = None
        steps = []
        for c in range(C):
            st = u[0, c, rows].astype(f32) + dual_step * coef[:, c * W : (c + 1) * W]
            steps.append(st)
            total = st * st if total is None else total + st * st
        scale = keep / jnp.maximum(jnp.sqrt(total), radius)
        for c in range(C):
            out[0, c, rows] = (steps[c] * scale).astype(bf16)


def step_kernel(
    C, FC, FR, R, W, B,
    u_hbm, x_hbm, d_hbm, wts_hbm, colT_hbm, row_taps, col_taps,
    new, ic, frows,
    u, x, d, wts, colT, spill, gcols, hrows, fcols,
    up, lo, dc, dcs, adj, adjs, radj, radjs,
    hown, hoth, wown, woth, back, bown, aown, aoth, pre,
    ext, exts, rmain, rsides, htop, hbot,
    send_u, recv_u, send_a, recv_a, send_as, recv_as,
    send_e, recv_e, send_es, recv_es, send_p, recv_p, send_h, recv_h, load,
):
    half = FC * W // 2
    me = lax.axis_index("chan")
    s = lax.axis_index("split")
    ma, mb = me % FR, me // FR
    has_up = (ma > 0) | (s == 1)
    has_down = (ma < FR - 1) | (s == 0)
    partner = {"chan": me, "split": 1 - s}
    down_id = {"chan": (me + s) % C, "split": 1 - s}
    up_id = {"chan": (me + s + C - 1) % C, "split": 1 - s}
    per = W // 16

    def remote(src, dst, ssem, rsem, device):
        return pltpu.make_async_remote_copy(
            src_ref=src, dst_ref=dst, send_sem=ssem, recv_sem=rsem,
            device_id=device, device_id_type=pl.DeviceIdType.MESH,
        )

    loads = [
        pltpu.make_async_copy(a, b, load.at[i])
        for i, (a, b) in enumerate(
            [(u_hbm, u), (colT_hbm, colT), (x_hbm, x), (wts_hbm, wts), (d_hbm, d)]
        )
    ]
    for copy in loads:
        copy.start()
    barrier = pltpu.get_barrier_semaphore()

    @pl.loop(1, C)
    def _(i):
        pl.semaphore_signal(
            barrier, inc=1, device_id={"chan": (me + i) % C, "split": s},
            device_id_type=pl.DeviceIdType.MESH,
        )

    pl.semaphore_signal(barrier, inc=1, device_id=partner, device_id_type=pl.DeviceIdType.MESH)
    if FR > 1:
        cross = jnp.where(s == 0, ma > 0, ma < FR - 1)
        cross_chan = jnp.where(s == 0, (me + C - 1) % C, (me + 1) % C)

        @pl.when(cross)
        def _():
            pl.semaphore_signal(
                barrier, inc=1, device_id={"chan": cross_chan, "split": 1 - s},
                device_id_type=pl.DeviceIdType.MESH,
            )
            pl.semaphore_wait(barrier, 1)

    adjoint_tables(W, B, row_taps, col_taps, gcols, hrows)
    loads[0].wait()
    pl.semaphore_wait(barrier, C)

    def chain(down_src, down_dst, up_src, up_dst, ssem, rsem):
        downward = remote(down_src, down_dst, ssem.at[0], rsem.at[0], down_id)
        upward = remote(up_src, up_dst, ssem.at[1], rsem.at[1], up_id)

        @pl.when(has_down)
        def _():
            downward.start()

        @pl.when(has_up)
        def _():
            upward.start()

        @pl.when(jnp.logical_not(has_up))
        def _():
            down_dst[...] = jnp.zeros_like(down_dst)

        @pl.when(jnp.logical_not(has_down))
        def _():
            up_dst[...] = jnp.zeros_like(up_dst)

        def finish():
            @pl.when(has_down)
            def _():
                downward.wait_send()
                upward.wait_recv()

            @pl.when(has_up)
            def _():
                upward.wait_send()
                downward.wait_recv()

        return finish

    finish_u = chain(u.at[:, :, pl.ds(R - PAD, PAD)], up, u.at[:, :, pl.ds(0, PAD)], lo, send_u, recv_u)
    loads[1].wait()
    table_body(s, FR, R, colT, bown, aown, aoth)
    finish_u()

    def peer(i):
        return (me + 1 + i) % C

    def send(buf, dst, ssem, rsem):
        def start(i):
            @pl.when(i < C - 1)
            def _():
                remote(
                    buf.at[i], dst.at[me], ssem.at[i], rsem.at[i], {"chan": peer(i), "split": s}
                ).start()

            @pl.when(i == C - 1)
            def _():
                dst[me] = buf[i]

        return start

    def finish(buf, dst, ssem, rsem):
        @pl.loop(0, C - 1)
        def _(i):
            remote(
                buf.at[i], dst.at[me], ssem.at[i], rsem.at[i], {"chan": peer(i), "split": s}
            ).wait()

    @pl.loop(0, C // per)
    def _(g):
        adjoint_group(
            R, W, B, g * per, peer, u, up, lo, gcols, hrows, adj, adjs, dc, dcs,
            send(adj, radj, send_a, recv_a), send(adjs, radjs, send_as, recv_as),
        )

    for copy in loads[2:]:
        copy.wait()
    step = 256
    chunks = half // step

    def to_partner(buf, dst, lanes, i):
        return remote(buf.at[:, lanes], dst.at[:, lanes], send_p.at[i], recv_p.at[i], partner)

    def parts(j):
        return pl.ds(j * step, step), pl.ds(half + j * step, step)

    copies = []
    for j in range(chunks):
        for q, lanes in enumerate(parts(j)):
            half_chunk(FC, x, colT, hown, lanes)
            copy = to_partner(hown, hoth, lanes, 2 * j + q)
            copy.start()
            copies.append(copy)
    spill_table(FC, W, spill)
    second = []
    for j in range(chunks):
        copies[2 * j].wait()
        copies[2 * j + 1].wait()
        vis_chunk(aown, aoth, hown, hoth, wts, wown, *parts(j))
        for q, lanes in enumerate(parts(j)):
            copy = to_partner(wown, woth, lanes, 2 * chunks + 2 * j + q)
            copy.start()
            second.append(copy)
    for j in range(chunks):
        second[2 * j].wait()
        second[2 * j + 1].wait()
        back_chunk(s, half, bown, wown, woth, back, *parts(j))
    gradient_body(FC, W, back, colT, x, d, pre)

    finish(adjs, radjs, send_as, recv_as)
    finish(adj, radj, send_a, recv_a)
    st = side_rows(FC, FR, radjs)
    k = lax.broadcasted_iota(jnp.int32, (2 * MARGIN, W), 0)
    col = lax.broadcasted_iota(jnp.int32, (2 * MARGIN, W), 1)
    take_left = jnp.where((k < MARGIN) & (col == W - MARGIN + k), 1.0, 0.0)
    take_right = jnp.where((k >= MARGIN) & (col == k - MARGIN), 1.0, 0.0)

    def deliver(buf, dst, ssem, rsem, i, start):
        b = (mb + i) % FC
        for j in range(FR):
            f = b * FR + (ma + j) % FR
            r = i * FR + j
            if r == 0:
                if start:
                    dst[me] = buf[f]
                continue
            copy = remote(buf.at[f], dst.at[me], ssem.at[r], rsem.at[r], {"chan": f, "split": s})
            if start:
                copy.start()
            else:
                copy.wait_send()

    def image_cell(i):
        b = (mb + i) % FC
        lanes = pl.ds(pl.multiple_of(b * W, W), W)
        pieces = [radj[b * FR + a] for a in range(FR)]
        main = jnp.concatenate(pieces, axis=0) if FR > 1 else pieces[0]
        upd = pre[:, lanes] - primal_step * (main.astype(f32) + dot(st, spill[:, lanes]))
        nb = jnp.maximum(upd, 0.0).astype(bf16)
        eb = (2.0 * nb.astype(f32) - x[b].astype(f32)).astype(bf16)
        new[b] = nb
        for a in range(FR):
            ext[b * FR + a] = eb[a * R : (a + 1) * R]
        deliver(ext, rmain, send_e, recv_e, i, True)

    def image_sides(i):
        b = (mb + i) % FC
        left = jnp.where(b > 0, take_left, 0.0).astype(bf16)
        right = jnp.where(b < FC - 1, take_right, 0.0).astype(bf16)
        nt = (((1,), (1,)), ((), ()))
        for a in range(FR):
            lf = (b + FC - 1) % FC * FR + a
            rf = (b + 1) % FC * FR + a
            both = lax.dot_general(left, ext[lf], nt, preferred_element_type=f32)
            both = both + lax.dot_general(right, ext[rf], nt, preferred_element_type=f32)
            exts[b * FR + a] = both.astype(bf16)
        deliver(exts, rsides, send_es, recv_es, i, True)

    for i in range(FC):
        image_cell(i)
        if i >= 2:
            image_sides(i - 1)
    image_sides(FC - 1)
    image_sides(0)
    forward_tables(W, B, row_taps, col_taps, fcols, frows)
    forward_cols(R, W, me, rmain, rsides, fcols, ic)
    for i in range(FC):
        for j in range(FR):
            r = i * FR + j
            if r == 0:
                continue
            src_b, src_a = (mb + FC - i) % FC, (ma + FR - j) % FR
            c = src_b * FR + src_a
            device = {"chan": c, "split": s}
            remote(exts.at[c], rsides.at[c], send_es.at[r], recv_es.at[r], device).wait_recv()
            remote(ext.at[c], rmain.at[c], send_e.at[r], recv_e.at[r], device).wait_recv()
            forward_cols(R, W, c, rmain, rsides, fcols, ic)
    for i in range(FC):
        deliver(exts, rsides, send_es, recv_es, i, False)
        deliver(ext, rmain, send_e, recv_e, i, False)
    finish_h = chain(
        ic.at[:, pl.ds(R, PAD)], htop, ic.at[:, pl.ds(PAD, PAD)], hbot, send_h, recv_h
    )
    finish_h()
    ic[:, :PAD] = htop[...]
    ic[:, PAD + R :] = hbot[...]


def per_device(sky_image, dirty_image, uv_weights, dual_coeffs, support_mask, row_taps, col_taps):
    FC, FR = sky_image.shape[1], sky_image.shape[2]
    R, W = sky_image.shape[4], sky_image.shape[5]
    C = dual_coeffs.shape[1]
    npix = FC * W
    half = npix // 2
    B = min(128, R)
    RP = R + 2 * PAD
    u = dual_coeffs.reshape(NB, C, R, W)
    x = sky_image.reshape(FC, FR * R, W)
    d = dirty_image.reshape(FC, FR * R, W)
    wts = uv_weights.reshape(half, half)
    mask = support_mask.reshape(R, W)
    colT = col_dft(npix)
    vm = lambda *shape: pltpu.VMEM(shape, bf16)
    sem = lambda n: pltpu.SemaphoreType.DMA((n,))
    any_spec = pl.BlockSpec(memory_space=pl.ANY)
    smem_spec = pl.BlockSpec(memory_space=pltpu.SMEM)
    span = B + 2 * PAD
    new, ic, frows = pl.pallas_call(
        functools.partial(step_kernel, C, FC, FR, R, W, B),
        out_shape=[
            jax.ShapeDtypeStruct((FC, FR * R, W), bf16),
            jax.ShapeDtypeStruct((NB, RP, C * W), bf16),
            jax.ShapeDtypeStruct((NB, B, span), bf16),
        ],
        in_specs=[any_spec] * 5 + [smem_spec] * 2,
        scratch_shapes=[
            vm(NB, C, R, W), vm(FC, FR * R, W), vm(FC, FR * R, W),
            pltpu.VMEM((half, half), jnp.int32), vm(npix, npix),
            vm(FC * 16, FC * W), vm(NB, W, 2 * W), vm(NB, B, span), vm(W + 16, NB * W),
            vm(NB, C, PAD, W), vm(NB, C, PAD, W), vm(NB, RP, 2 * W), vm(NB, RP, W),
            vm(C, R, W), vm(C, 16, R), vm(C, R, W), vm(C, 16, R),
            *[vm(half, npix)] * 8, pltpu.VMEM((half, npix), f32),
            vm(C, R, W), vm(C, 16, R), vm(C, R, W), vm(C, 16, R),
            vm(NB, PAD, C * W), vm(NB, PAD, C * W),
            sem(2), sem(2), sem(C), sem(C), sem(C), sem(C),
            sem(C), sem(C), sem(C), sem(C), sem(4 * half // 128), sem(4 * half // 128), sem(2), sem(2), sem(5),
        ],
        compiler_params=pltpu.CompilerParams(
            collective_id=0, has_side_effects=True, vmem_limit_bytes=58 * 2**20
        ),
    )(u, x, d, wts, colT, row_taps, col_taps)

    part = FC // NB
    new_dual, new = pl.pallas_call(
        functools.partial(shrink_body, C, R, W, B),
        grid=(NB,),
        in_specs=[
            pl.BlockSpec((1, RP, C * W), lambda n: (n, 0, 0)),
            pl.BlockSpec((1, B, B + 2 * PAD), lambda n: (n, 0, 0)),
            pl.BlockSpec((1, C, R, W), lambda n: (n, 0, 0, 0)),
            pl.BlockSpec((R, W), lambda n: (0, 0)),
            pl.BlockSpec((part, FR * R, W), lambda n: (n, 0, 0)),
        ],
        out_specs=[
            pl.BlockSpec((1, C, R, W), lambda n: (n, 0, 0, 0)),
            pl.BlockSpec((part, FR * R, W), lambda n: (n, 0, 0)),
        ],
        out_shape=[
            jax.ShapeDtypeStruct((NB, C, R, W), bf16),
            jax.ShapeDtypeStruct((FC, FR * R, W), bf16),
        ],
    )(ic, frows, u, mask, new)
    return (new.reshape(sky_image.shape), new_dual.reshape(dual_coeffs.shape))


def solution(mesh):
    placed = (
        P(("cube", "chan"), None, None, "split", None, None),
        P(("cube", "chan"), None, None, "split", None, None),
        P(("cube", "chan"), "split", None),
        P(None, "cube", "chan", "split", None, None),
        P("chan", "split", None, None),
        P(),
        P(),
    )
    return jax.shard_map(
        per_device,
        mesh=mesh,
        in_specs=placed,
        out_specs=(
            P(("cube", "chan"), None, None, "split", None, None),
            P(None, "cube", "chan", "split", None, None),
        ),
        check_vma=False,
    )
```

time: 94.4 us -> 78.2 us (0.83)
  the two profiles are of different devices: /device:TPU:0 before, /device:TPU:25 now
where the time goes in v2:
time: 78.2 us; the launch traced here: 78 us
  Pallas kernels  77.3 us (99%)
    pallas_call x1, Pallas kernels, per_device(): pl.pallas_call(functools.partial(step_kernel, C, FC, FR, R, W, B), out_sh...  69.3 us
    pallas_call x1, Pallas kernels, per_device(): pl.pallas_call(functools.partial(shrink_body, C, R, W, B), grid=(NB,), in...  8.03 us

profile of v2, /device:TPU:25, one launch (start us, length us, event | category | flops | bytes accessed | tf_op | source)
XLA Modules:
  0.0 78.0 jit_solution(1260261054590585807)
XLA Ops:
  0.6 69.3 %shard_map.95 = (bf16[8,512,128]{2,1,0:T(8,128)(2,1)}, bf16[4,544,1024]{2,1,0:T(8,128)(2,1)}, bf16[4,128,160]{2,1,0:T(8,128)(2,1)}) custom-call(bf16[4,8,512,128]{3,2,1,0:T(8,128)(2,1)} %bitcast.11, bf16[8,512,128]{2,1,0:T(8,128)(2,1)} %bitcast.13, bf16[8,512,128]{2,1,0:T(8,128)(2,1)} %bitcast.14, s32[512,512]{1,0:T(8,128)} %bitcast.15, ...), custom_call_target="tpu_custom_call" | custom-call | tf_op jit(solution)/shard_map/pallas_call | solution.py:491
  70.0 8.0 %shard_map.96 = (bf16[4,8,512,128]{3,2,1,0:T(8,128)(2,1)}, bf16[8,512,128]{2,1,0:T(8,128)(2,1)}) custom-call(bf16[4,544,1024]{2,1,0:T(8,128)(2,1)} %get-tuple-element.7.ic, bf16[4,128,160]{2,1,0:T(8,128)(2,1)} %get-tuple-element.8.frows, bf16[4,8,512,128]{3,2,1,0:T(8,128)(2,1)} %bitcast.12, s32[512,128]{1,0:T(8,128)} %bitcast.16, ...), custom_call_target="tpu_custom_call" | custom-call | tf_op jit(solution)/shard_map/pallas_call | solution.py:517

commit v3 on v2

--- a/solution.py
+++ b/solution.py
@@ -326,7 +326,7 @@
     finish_u()
 
     def peer(i):
-        return (me + 1 + i) % C
+        return (me + C // 2 + (i + 1) // 2 * (1 - 2 * (i % 2))) % C
 
     def send(buf, dst, ssem, rsem):
         def start(i):
@@ -439,15 +439,18 @@
             exts[b * FR + a] = both.astype(bf16)
         deliver(exts, rsides, send_es, recv_es, i, True)
 
-    for i in range(FC):
+    order = [FC // 2 + (i + 1) // 2 * (1 - 2 * (i % 2)) for i in range(FC)]
+    ready, sided = set(), set()
+    for i in order:
         image_cell(i)
-        if i >= 2:
-            image_sides(i - 1)
-    image_sides(FC - 1)
-    image_sides(0)
+        ready.add(i)
+        for k in order:
+            if k not in sided and {(k + 1) % FC, (k - 1) % FC} <= ready:
+                image_sides(k)
+                sided.add(k)
     forward_tables(W, B, row_taps, col_taps, fcols, frows)
     forward_cols(R, W, me, rmain, rsides, fcols, ic)
-    for i in range(FC):
+    for i in order:
         for j in range(FR):
             r = i * FR + j
             if r == 0:

time: 78.2 us -> 77.6 us (level)
  the two profiles are of different devices: /device:TPU:25 before, /device:TPU:0 now
where the time goes in v3:
time: 77.6 us; the launch traced here: 77.5 us
  Pallas kernels  76.8 us (99%)
    pallas_call x1, Pallas kernels, per_device(): pl.pallas_call(functools.partial(step_kernel, C, FC, FR, R, W, B), out_sh...  68.8 us
    pallas_call x1, Pallas kernels, per_device(): pl.pallas_call(functools.partial(shrink_body, C, R, W, B), grid=(NB,), in...  8.03 us

profile of v3, /device:TPU:0, one launch (start us, length us, event | category | flops | bytes accessed | tf_op | source)
XLA Modules:
  0.0 77.5 jit_solution(11948685915418317743)
XLA Ops:
  0.6 68.8 %shard_map.95 = (bf16[8,512,128]{2,1,0:T(8,128)(2,1)}, bf16[4,544,1024]{2,1,0:T(8,128)(2,1)}, bf16[4,128,160]{2,1,0:T(8,128)(2,1)}) custom-call(bf16[4,8,512,128]{3,2,1,0:T(8,128)(2,1)} %bitcast.11, bf16[8,512,128]{2,1,0:T(8,128)(2,1)} %bitcast.13, bf16[8,512,128]{2,1,0:T(8,128)(2,1)} %bitcast.14, s32[512,512]{1,0:T(8,128)} %bitcast.15, ...), custom_call_target="tpu_custom_call" | custom-call | tf_op jit(solution)/shard_map/pallas_call | solution.py:494
  69.4 8.0 %shard_map.96 = (bf16[4,8,512,128]{3,2,1,0:T(8,128)(2,1)}, bf16[8,512,128]{2,1,0:T(8,128)(2,1)}) custom-call(bf16[4,544,1024]{2,1,0:T(8,128)(2,1)} %get-tuple-element.7.ic, bf16[4,128,160]{2,1,0:T(8,128)(2,1)} %get-tuple-element.8.frows, bf16[4,8,512,128]{3,2,1,0:T(8,128)(2,1)} %bitcast.12, s32[512,128]{1,0:T(8,128)} %bitcast.16, ...), custom_call_target="tpu_custom_call" | custom-call | tf_op jit(solution)/shard_map/pallas_call | solution.py:520
